TPU v7x, 512 devices: a whole 4x8x8 slice. The times are simulated.
512 devices in a mesh: fsdp: 64 (over x, z, y_hi), dp: 8 (over y_lo, core).
Axes of the slice: x: 4, y: 8 (y_hi: 2, y_lo: 4; y = y_hi * 4 + y_lo), z: 8, core: 2. Of those that a mesh axis runs over, the one named last changes fastest.
Arguments:
- tokens: bfloat16 [65536, 8192], P(('fsdp', 'dp')), may hold values from -6 to 6
- token_adapter_index: int32 [65536, 1], P(('fsdp', 'dp')), may hold values from 0 to 63; in each aligned block of 128 rows (0 to 127, 128 to 255, ...) at most 3 rows name the same one
- adapter_storage_index: int32 [64], replicated, may hold values from 0 to 63, each once
- frozen_value_weight: bfloat16 [8192, 512], P(('fsdp', 'dp')), may hold values from -0.0625 to 0.0625
- frozen_value_bias: bfloat16 [512], replicated, may hold values from -3 to 3
- adapter_down_weight: bfloat16 [64, 8192, 64], P('fsdp'), may hold values from -0.0625 to 0.0625
- adapter_up_weight: bfloat16 [64, 64, 512], P('fsdp'), may hold values from -0.75 to 0.75
- cotangent: bfloat16 [65536, 512], P(('fsdp', 'dp')), may hold values from -0.1875 to 0.1875
Outputs:
- values: bfloat16 [65536, 512], P(('fsdp', 'dp'))
- grad_down: float32 [64, 8192, 64], P('fsdp', 'dp')
- grad_up: float32 [64, 64, 512], P('fsdp', None, 'dp')
Inputs may be any that keep to these rules, and one draw needn't show every extreme that they name: `token_adapter_index`: within the 128 rows of one device no adapter is named by more than 3 rows. `adapter_storage_index`: each storage index appears once.
All inputs are finite; a program needn't handle non-finite values.
Results may differ from a plain program's by a relative error of at most 0.0048.
Values may be sent and summed in bfloat16 or wider, within the bound.
No kernel may reach another device: no remote copies, remote signals or barrier semaphores. Data moves between devices by JAX's collectives and lax.ppermute only.
A program may use at most 64 MiB of HBM per device.

v0:
```python
import jax
import jax.numpy as jnp
from jax import lax
from jax.sharding import PartitionSpec as P


def body(
    tokens,
    token_adapter_index,
    adapter_storage_index,
    frozen_value_weight,
    frozen_value_bias,
    adapter_down_weight,
    adapter_up_weight,
    cotangent,
):
    token_count, model_width = tokens.shape
    value_width = frozen_value_weight.shape[1]
    fsdp_size = lax.axis_size("fsdp")
    slots_total = adapter_storage_index.shape[0]
    capacity = max(2, (3 * token_count + 2 * fsdp_size - 1) // (2 * fsdp_size))
    base_value = jnp.dot(
        tokens,
        lax.all_gather(frozen_value_weight, ("fsdp", "dp"), axis=0, tiled=True),
        preferred_element_type=jnp.float32,
    )
    base_value = base_value + frozen_value_bias.astype(jnp.float32)
    owner_index = jnp.take(adapter_storage_index, token_adapter_index[:, 0])
    onehot = (owner_index[:, None] == jnp.arange(slots_total)[None, :]).astype(jnp.int32)
    place_in_slot = jnp.sum((jnp.cumsum(onehot, 0) - onehot) * onehot, 1)
    target_row = owner_index * capacity + place_in_slot
    dispatch = (jnp.arange(slots_total * capacity)[:, None] == target_row[None, :]).astype(
        jnp.bfloat16
    )
    sent_rows = jnp.dot(dispatch, tokens, preferred_element_type=jnp.float32).astype(jnp.bfloat16)
    sent_rows = sent_rows.reshape(slots_total, capacity, model_width)
    sent_cot = jnp.dot(dispatch, cotangent, preferred_element_type=jnp.float32).astype(jnp.bfloat16)
    sent_cot = sent_cot.reshape(slots_total, capacity, value_width)
    arrived = lax.all_to_all(sent_rows, "fsdp", split_axis=0, concat_axis=0, tiled=True)
    arrived_rows = arrived.reshape(-1, model_width)
    down_projection = adapter_down_weight[0]
    up_projection = adapter_up_weight[0]
    rank_activation = jnp.dot(
        arrived_rows, down_projection, preferred_element_type=jnp.float32
    ).astype(jnp.bfloat16)
    adapter_delta = jnp.dot(
        rank_activation, up_projection, preferred_element_type=jnp.float32
    ).astype(jnp.bfloat16)
    returned = lax.all_to_all(
        adapter_delta.reshape(fsdp_size, capacity, value_width),
        "fsdp",
        split_axis=0,
        concat_axis=0,
        tiled=True,
    )
    returned = returned.reshape(-1, value_width)
    placed = jnp.einsum("st,sk->tk", dispatch, returned, preferred_element_type=jnp.float32)
    values = (base_value + placed).astype(jnp.bfloat16)
    arrived_cot = lax.all_to_all(sent_cot, "fsdp", split_axis=0, concat_axis=0, tiled=True)
    cotangent_rows = arrived_cot.reshape(-1, value_width)
    rank_cotangent = lax.dot_general(
        cotangent_rows, up_projection, (((1,), (1,)), ((), ())), preferred_element_type=jnp.float32
    ).astype(jnp.bfloat16)
    grad_down = lax.dot_general(
        arrived_rows, rank_cotangent, (((0,), (0,)), ((), ())), preferred_element_type=jnp.float32
    )
    grad_up = lax.dot_general(
        rank_activation,
        cotangent_rows,
        (((0,), (0,)), ((), ())),
        preferred_element_type=jnp.float32,
    )
    summed_down, summed_up = (
        lax.psum_scatter(grad_down, "dp", scatter_dimension=0, tiled=True),
        lax.psum_scatter(grad_up, "dp", scatter_dimension=1, tiled=True),
    )
    return (values, summed_down[None], summed_up[None])


def solution(mesh):
    return jax.shard_map(
        body,
        mesh=mesh,
        in_specs=(
            P(("fsdp", "dp"), None),
            P(("fsdp", "dp"), None),
            P(),
            P(("fsdp", "dp"), None),
            P(),
            P("fsdp", None, None),
            P("fsdp", None, None),
            P(("fsdp", "dp"), None),
        ),
        out_specs=(P(("fsdp", "dp"), None), P("fsdp", "dp", None), P("fsdp", None, "dp")),
        check_vma=False,
    )
```

profile of v0, /device:TPU:1, one launch (start us, length us, event | category | flops | bytes accessed | tf_op | source)
XLA Modules:
  0.0 325.9 jit_solution(2407330163752891406)
XLA Ops:
  8.0 0.0 copy-start
  8.0 0.8 fusion.13
  8.8 1.6 gather_fusion
  10.4 0.7 fusion.12
  11.1 0.1 fusion.6
  11.2 0.2 reduce_window_sum.11
  11.3 0.2 select_reduce_fusion
  11.5 0.7 fusion.11
  12.2 1.1 convolution_convert_fusion.2
  13.3 0.8 reshape.45
  14.1 19.6 %all-to-all-start.2 = ((bf16[64,3,512]{2,1,0:T(4,128)(2,1)}), bf16[64,3,512]{2,1,0:T(4,128)(2,1)S(1)}, u32[]{:S(2)}, u32[]{:S(2)}) async-start(bf16[64,3,512]{2,1,0:T(4,128)(2,1)} %reshape.45), calls=%async_computation.2 | async-start | bytes 524288 | tf_op jit(solution)/shard_map/all_to_all | solution.py:59
  33.7 0.0 copy-done
  33.7 2.6 convolution_convert_fusion
  36.3 7.1 %reshape.41 = bf16[64,3,8192]{2,1,0:T(4,128)(2,1)} reshape(bf16[192,8192]{1,0:T(8,128)(2,1)} %convolution_convert_fusion) | data formatting | bytes 6291456 | tf_op jit(solution)/shard_map/reshape | solution.py:36
  43.4 4.0 %all-to-all-done.2 = bf16[64,3,512]{2,1,0:T(4,128)(2,1)S(1)} async-done(((bf16[64,3,512]{2,1,0:T(4,128)(2,1)}), bf16[64,3,512]{2,1,0:T(4,128)(2,1)S(1)}, u32[]{:S(2)}, u32[]{:S(2)}) %all-to-all-start.2) | async-done | bytes 196640 | tf_op jit(solution)/shard_map/all_to_all | solution.py:59
  47.4 10.9 %all-to-all-start = ((bf16[64,3,8192]{2,1,0:T(4,128)(2,1)}), bf16[64,3,8192]{2,1,0:T(4,128)(2,1)}, u32[]{:S(2)}, u32[]{:S(2)}) async-start(bf16[64,3,8192]{2,1,0:T(4,128)(2,1)} %reshape.41), calls=%async_computation | async-start | bytes 8388608 | tf_op jit(solution)/shard_map/all_to_all | solution.py:39
  58.2 0.0 reduce-scatter.7.cloned.1.call-start
  58.3 0.2 reshape.46
  58.5 0.0 copy-start.1
  58.5 94.7 %all-to-all-done = bf16[64,3,8192]{2,1,0:T(4,128)(2,1)} async-done(((bf16[64,3,8192]{2,1,0:T(4,128)(2,1)}), bf16[64,3,8192]{2,1,0:T(4,128)(2,1)}, u32[]{:S(2)}, u32[]{:S(2)}) %all-to-all-start) | async-done | bytes 3145760 | tf_op jit(solution)/shard_map/all_to_all | solution.py:39
  153.1 7.5 %reshape.42 = bf16[192,8192]{1,0:T(8,128)(2,1)} reshape(bf16[64,3,8192]{2,1,0:T(4,128)(2,1)} %all-to-all-done) | data formatting | bytes 6291456 | tf_op jit(solution)/shard_map/reshape | solution.py:40
  160.6 0.0 copy-done.1
  160.6 0.0 copy-start.2
  160.6 3.0 convolution_convert_fusion.4
  163.6 1.0 convolution_bitcast_fusion
  164.6 0.0 reduce-scatter.7.cloned.1.call-update
  164.6 0.0 all-gather.2.cloned.1.call-start
  164.7 0.5 all-gather.2.cloned.1.call-update
  165.2 0.0 copy-start.3
  165.2 0.0 reduce-scatter.5.cloned.1.call-start
  165.3 0.0 copy-done.2
  165.3 4.2 %fusion.1 = f32[8192,64]{0,1:T(8,128)} fusion(bf16[192,8192]{1,0:T(8,128)(2,1)} %reshape.42, bf16[192,512]{1,0:T(8,128)(2,1)S(1)} %reshape.46, bf16[1,64,512]{2,1,0:T(8,128)(2,1)S(1)} %copy-done.2), kind=kOutput, calls=%fused_computation.10 | convolution fusion | flops 213921792 | bytes 5505024 | tf_op jit(solution)/shard_map/dot_general | solution.py:64
  169.5 0.0 reduce-scatter.5.cloned.1.call-update
  169.6 0.2 convolution_convert_fusion.1
  169.8 0.8 reshape.43
  170.7 13.7 %all-to-all-start.1 = ((bf16[64,3,512]{2,1,0:T(4,128)(2,1)}), bf16[64,3,512]{2,1,0:T(4,128)(2,1)S(1)}, u32[]{:S(2)}, u32[]{:S(2)}) async-start(bf16[64,3,512]{2,1,0:T(4,128)(2,1)} %reshape.43), calls=%async_computation.1 | async-start | bytes 524288 | tf_op jit(solution)/shard_map/all_to_all | solution.py:49
  184.4 0.0 copy-done.3
  184.4 31.2 %reduce-scatter.7.cloned.1.call-done = f32[64,64]{1,0:T(8,128)} async-done(((f32[512,64]{1,0:T(8,128)}), f32[64,64]{1,0:T(8,128)}) %reduce-scatter.7.cloned.1.call-update) | async-done | bytes 16400
  215.6 1.5 copy.12
  217.1 0.0 all-to-all-done.1
  217.1 0.2 reshape.44
  217.2 95.7 %all-gather.2.cloned.1.call-done = bf16[8192,512]{1,0:T(8,128)(2,1)} async-done(((bf16[16,512]{1,0:T(8,128)(2,1)}), bf16[8192,512]{1,0:T(8,128)(2,1)}) %all-gather.2.cloned.1.call-update) | async-done | bytes 8388624 | tf_op jit(solution)/shard_map/all_gather | solution.py:24
  312.9 4.6 %convolution_add_fusion.1 = f32[128,512]{1,0:T(8,128)S(1)} fusion(bf16[128,8192]{1,0:T(8,128)(2,1)S(1)} %copy-done, bf16[8192,512]{1,0:T(8,128)(2,1)} %all-gather.2.cloned.1.call-done, f32[512]{0:T(512)S(1)} %convert_element_type.25), kind=kOutput, calls=%fused_computation.6 | convolution fusion | flops 1073807360 | bytes 10749952 | tf_op jit(solution)/shard_map/dot_general | solution.py:22
  317.6 0.9 fusion
  318.4 0.0 reduce-scatter.5.cloned.1.call-done
  (2 shorter events, 0.0 us)
Async XLA Ops:
  8.0 25.7 %copy-start = (bf16[128,8192]{1,0:T(8,128)(2,1)S(1)}, bf16[128,8192]{1,0:T(8,128)(2,1)}, u32[]{:S(2)}) copy-start(bf16[128,8192]{1,0:T(8,128)(2,1)} %param.8) | copy-start | bytes 6291460
  14.1 33.3 %all-to-all-start.2 = ((bf16[64,3,512]{2,1,0:T(4,128)(2,1)}), bf16[64,3,512]{2,1,0:T(4,128)(2,1)S(1)}, u32[]{:S(2)}, u32[]{:S(2)}) async-start(bf16[64,3,512]{2,1,0:T(4,128)(2,1)} %reshape.45), calls=%async_computation.2 | async-start | bytes 524288 | tf_op jit(solution)/shard_map/all_to_all | solution.py:59
  47.4 105.8 %all-to-all-start = ((bf16[64,3,8192]{2,1,0:T(4,128)(2,1)}), bf16[64,3,8192]{2,1,0:T(4,128)(2,1)}, u32[]{:S(2)}, u32[]{:S(2)}) async-start(bf16[64,3,8192]{2,1,0:T(4,128)(2,1)} %reshape.41), calls=%async_computation | async-start | bytes 8388608 | tf_op jit(solution)/shard_map/all_to_all | solution.py:39
  58.2 157.4 %reduce-scatter.7.cloned.1.call-start = ((), (), s32[]{:S(2)}) async-start(), calls=%async_computation.7 | async-start | bytes 294912
  58.5 102.1 %copy-start.1 = (bf16[1,8192,64]{1,2,0:T(8,128)(2,1)S(1)}, bf16[1,8192,64]{1,2,0:T(8,128)(2,1)}, u32[]{:S(2)}) copy-start(bf16[1,8192,64]{1,2,0:T(8,128)(2,1)} %param.13) | copy-start | bytes 3145732
  160.6 4.7 %copy-start.2 = (bf16[1,64,512]{2,1,0:T(8,128)(2,1)S(1)}, bf16[1,64,512]{2,1,0:T(8,128)(2,1)}, u32[]{:S(2)}) copy-start(bf16[1,64,512]{2,1,0:T(8,128)(2,1)} %param.14) | copy-start | bytes 196612
  164.6 148.3 %all-gather.2.cloned.1.call-start = ((), (), s32[]{:S(2)}) async-start(), calls=%async_computation.5 | async-start | bytes 8404992 | tf_op jit(solution)/shard_map/all_gather | solution.py:24
  165.2 19.1 %copy-start.3 = (bf16[512]{0:T(512)(128)(2,1)S(1)}, bf16[512]{0:T(512)(128)(2,1)}, u32[]{:S(2)}) copy-start(bf16[512]{0:T(512)(128)(2,1)} %param.12) | copy-start | bytes 3076
  165.2 153.2 %reduce-scatter.5.cloned.1.call-start = ((), (), s32[]{:S(2)}) async-start(), calls=%async_computation.6 | async-start | bytes 2359296 | tf_op jit(solution)/shard_map/reduce_scatter | solution.py:74
  170.7 46.4 %all-to-all-start.1 = ((bf16[64,3,512]{2,1,0:T(4,128)(2,1)}), bf16[64,3,512]{2,1,0:T(4,128)(2,1)S(1)}, u32[]{:S(2)}, u32[]{:S(2)}) async-start(bf16[64,3,512]{2,1,0:T(4,128)(2,1)} %reshape.43), calls=%async_computation.1 | async-start | bytes 524288 | tf_op jit(solution)/shard_map/all_to_all | solution.py:49
Sparse Core Ops, SparseCore 0:
  164.8 50.7 reduce-scatter.6
  219.0 43.4 reduce-scatter.4
Sparse Core Ops, SparseCore 1:
  169.6 143.3 all-gather.1
where the time goes:
time: 327 us; the launch traced here: 326 us
  waiting for transfers between devices  226 us (69%)
  starting transfers between devices  44.3 us (14%)
  local copies, waits for them, and re-layouts  19.6 us (6%)
  matrix products  17.7 us (5%)
  between operations  15.6 us (5%)
    all_gather x1, waiting for transfers between devices, body(): lax.all_gather(frozen_value_weight, ('fsdp', 'dp'), axis=0, tiled=True)  95.7 us
    all_to_all x1, waiting for transfers between devices, body(): lax.all_to_all(sent_rows, 'fsdp', split_axis=0, concat_axis=0, tiled=True)  94.7 us
    unnamed x4, waiting for transfers between devices  31.8 us
    all_to_all x1, starting transfers between devices, body(): lax.all_to_all(sent_cot, 'fsdp', split_axis=0, concat_axis=0, tiled=True)  19.6 us
    all_to_all x1, starting transfers between devices, body(): lax.all_to_all(adapter_delta.reshape(fsdp_size, capacity, value_width), '...  13.7 us
    all_to_all x1, starting transfers between devices, body(): lax.all_to_all(sent_rows, 'fsdp', split_axis=0, concat_axis=0, tiled=True)  10.9 us
    reshape x1, local copies, waits for them, and re-layouts, body(): arrived_rows = arrived.reshape(-1, model_width)  7.46 us
    reshape x1, local copies, waits for them, and re-layouts, body(): sent_rows = sent_rows.reshape(slots_total, capacity, model_width)  7.05 us
  transfers between devices with their start and end apart: 6, of which 4 were waited for; matrix products, arithmetic and copies ran while one was open for 7% of the time, Pallas kernels for 0%

commit v1 on v0

v1 whole, which is shorter than its diff:
```python
import jax
import jax.numpy as jnp
from jax import lax
from jax.experimental import pallas as pl
from jax.experimental.pallas import tpu as pltpu
from jax.sharding import PartitionSpec as P

SLOTS = 3
Q = 8
F32 = jnp.float32
BF16 = jnp.bfloat16


def iota(shape, dimension):
    return lax.broadcasted_iota(jnp.int32, shape, dimension)


def nn(a, b):
    return lax.dot_general(a, b, (((1,), (0,)), ((), ())), preferred_element_type=F32)


def nt(a, b):
    return lax.dot_general(a, b, (((1,), (1,)), ((), ())), preferred_element_type=F32)


def tn(a, b):
    return lax.dot_general(a, b, (((0,), (0,)), ((), ())), preferred_element_type=F32)


def dispatch_kernel(storage_ref, index_ref, tokens_ref, cot_ref, sent_ref, place_ref, pick_ref):
    count, width = tokens_ref.shape
    rows = sent_ref.shape[0]
    chunk = width // Q
    half = cot_ref.shape[1] // 2
    index = index_ref[...]
    owner = jnp.zeros_like(index)
    for n in range(rows // Q):
        owner = jnp.where(index == n, storage_ref[n], owner)
    row = iota((rows, count), 0)
    q = row % Q
    mine = (row // Q) == jnp.broadcast_to(owner, (rows, count))
    mine_f = jnp.where(mine, 1.0, 0.0).astype(F32)
    earlier = jnp.where(iota((count, count), 0) < iota((count, count), 1), 1.0, 0.0).astype(BF16)
    rank = nn(mine_f.astype(BF16), earlier).astype(jnp.int32)
    for s in range(SLOTS):
        here = mine & (rank == s)
        for i in range(Q):
            pick_ref[s, :, i * count : (i + 1) * count] = jnp.where(
                here & (q == i), 1.0, 0.0
            ).astype(BF16)
    for h in range(2):
        both = mine & (rank == q // 2) & (q % 2 == h)
        place_ref[h] = jnp.where(both, 1.0, 0.0).astype(BF16)
        sent = nn(place_ref[h], cot_ref[:, h * half : (h + 1) * half])
        if h == 0:
            total = sent
        else:
            total = total + sent
    sent_ref[:, SLOTS * chunk :] = total.astype(BF16)
    step = 256

    @pl.loop(0, chunk // step)
    def _(block):
        start = block * step
        piece = jnp.concatenate(
            [
                tokens_ref[:, pl.ds(pl.multiple_of(i * chunk + start, step), step)]
                for i in range(Q)
            ],
            axis=0,
        )
        for s in range(SLOTS):
            sent_ref[:, pl.ds(pl.multiple_of(s * chunk + start, step), step)] = nn(
                pick_ref[s], piece
            ).astype(BF16)


def fold(masked, rank):
    rows, wide = masked.shape
    total = masked[:, : 2 * rank]
    for k in range(1, wide // (2 * rank)):
        total = total + masked[:, 2 * rank * k : 2 * rank * (k + 1)]
    total = total + pltpu.roll(total, rank, 1)
    total = jnp.sum(total.reshape(rows // Q, Q, 2 * rank), axis=1, keepdims=True)
    return jnp.broadcast_to(total, (rows // Q, Q, 2 * rank)).reshape(rows, 2 * rank)


def stacked_up(up_ref):
    half = up_ref.shape[1] // 2
    return jnp.concatenate([up_ref[:, :half], up_ref[:, half:]], axis=0)


def correct_kernel(arrived_ref, down_ref, up_ref, back_ref, low_ref):
    rows = arrived_ref.shape[0]
    rank, width = down_ref.shape
    chunk = width // Q
    q = iota((rows, 2 * rank), 0) % Q
    part = iota((rows, 2 * rank), 1) // rank
    wide_q = iota((rows, Q * rank), 0) % Q == iota((rows, Q * rank), 1) // rank
    down = jnp.concatenate([down_ref[:, i * chunk : (i + 1) * chunk] for i in range(Q)], axis=0)
    low = jnp.zeros((rows, 2 * rank), F32)
    for s in range(SLOTS):
        full = nt(arrived_ref[:, s * chunk : (s + 1) * chunk], down)
        low = jnp.where(q // 2 == s, fold(jnp.where(wide_q, full, 0.0), rank), low)
    low = jnp.where(part == q % 2, low, 0.0).astype(BF16)
    low_ref[...] = low
    back_ref[...] = nn(low, stacked_up(up_ref)).astype(BF16)


def grads_kernel(arrived_ref, up_ref, low_ref, grad_ref):
    rows = arrived_ref.shape[0]
    rank = up_ref.shape[0]
    chunk = grad_ref.shape[1] - 2 * rank
    cot = arrived_ref[:, SLOTS * chunk :]
    q = iota((rows, 2 * rank), 0) % Q
    part = iota((rows, 2 * rank), 1) // rank
    wide_q = iota((rows, Q * rank), 0) % Q == iota((rows, Q * rank), 1) // rank
    both = nt(cot, stacked_up(up_ref))
    lefts = []
    for s in range(SLOTS):
        back = fold(jnp.where((q // 2 == s) & (part == q % 2), both, 0.0), rank)
        lefts.append(
            jnp.where(wide_q, jnp.concatenate([back] * (Q // 2), axis=1), 0.0).astype(BF16)
        )
    left = jnp.concatenate(lefts, axis=0)
    step = 256
    for start in range(0, chunk, step):
        right = jnp.concatenate(
            [
                arrived_ref[:, s * chunk + start : s * chunk + start + step]
                for s in range(SLOTS)
            ],
            axis=0,
        )
        grad_ref[:, start : start + step] = tn(left, right).astype(BF16)
    up = tn(low_ref[...], cot).astype(BF16)
    per_half = Q // 2
    for d in range(Q):
        column = (d % per_half) // 2 * 2 * rank
        first = d // per_half * rank
        grad_ref[d * rank : (d + 1) * rank, chunk:] = up[
            first : first + rank, column : column + 2 * rank
        ]


def place_kernel(base0_ref, base1_ref, place_ref, back_ref, values_ref):
    half = back_ref.shape[1]
    for h, base_ref in enumerate((base0_ref, base1_ref)):
        placed = tn(place_ref[h], back_ref[...])
        values_ref[:, h * half : (h + 1) * half] = (base_ref[...] + placed).astype(BF16)


def vmem(number):
    return [pl.BlockSpec(memory_space=pltpu.VMEM)] * number


PARAMS = pltpu.CompilerParams(vmem_limit_bytes=48 << 20)


def body(
    tokens,
    token_adapter_index,
    adapter_storage_index,
    frozen_value_weight,
    frozen_value_bias,
    adapter_down_weight,
    adapter_up_weight,
    cotangent,
):
    count, width = tokens.shape
    out_width = frozen_value_weight.shape[1]
    fsdp = lax.axis_size("fsdp")
    dp = lax.axis_size("dp")
    rank = adapter_up_weight.shape[1]
    half = out_width // 2
    chunk = width // Q
    rows = fsdp * Q
    columns = SLOTS * chunk + half

    weights = []
    for h in range(2):
        weights.append(
            lax.all_gather(
                frozen_value_weight[:, h * half : (h + 1) * half],
                ("fsdp", "dp"),
                axis=0,
                tiled=True,
            )
        )
    sent, place = pl.pallas_call(
        dispatch_kernel,
        out_shape=(
            jax.ShapeDtypeStruct((rows, columns), BF16),
            jax.ShapeDtypeStruct((2, rows, count), BF16),
        ),
        in_specs=[pl.BlockSpec(memory_space=pltpu.SMEM)] + vmem(3),
        out_specs=tuple(vmem(2)),
        scratch_shapes=[pltpu.VMEM((SLOTS, rows, Q * count), BF16)],
        compiler_params=PARAMS,
        name="dispatch",
    )(adapter_storage_index, token_adapter_index.reshape(1, count), tokens, cotangent)
    arrived = lax.all_to_all(
        sent.reshape(fsdp, Q, columns), "fsdp", split_axis=0, concat_axis=0, tiled=True
    ).reshape(rows, columns)
    down = jnp.swapaxes(adapter_down_weight[0], 0, 1)
    up = adapter_up_weight[0]
    back, low = pl.pallas_call(
        correct_kernel,
        out_shape=(
            jax.ShapeDtypeStruct((rows, half), BF16),
            jax.ShapeDtypeStruct((rows, 2 * rank), BF16),
        ),
        in_specs=vmem(3),
        out_specs=tuple(vmem(2)),
        compiler_params=PARAMS,
        name="correct",
    )(arrived, down, up)
    back = lax.all_to_all(
        back.reshape(fsdp, Q, half), "fsdp", split_axis=0, concat_axis=0, tiled=True
    ).reshape(rows, half)
    grads = pl.pallas_call(
        grads_kernel,
        out_shape=jax.ShapeDtypeStruct((dp * rank, chunk + 2 * rank), BF16),
        in_specs=vmem(3),
        out_specs=vmem(1)[0],
        compiler_params=PARAMS,
        name="grads",
    )(arrived, up, low)
    grads = lax.all_to_all(
        grads.reshape(dp, rank, chunk + 2 * rank),
        "dp",
        split_axis=0,
        concat_axis=0,
        tiled=True,
    )
    grads = jnp.sum(grads.astype(F32), axis=0)
    odd = lax.axis_index("dp") % 2 == 1
    grad_up = jnp.where(odd, grads[:, chunk + rank :], grads[:, chunk : chunk + rank])
    grad_down = jnp.swapaxes(grads[:, :chunk], 0, 1)
    base = [
        jnp.dot(tokens, weights[h], preferred_element_type=F32)
        + frozen_value_bias[h * half : (h + 1) * half].astype(F32)
        for h in range(2)
    ]
    values = pl.pallas_call(
        place_kernel,
        out_shape=jax.ShapeDtypeStruct((count, out_width), BF16),
        in_specs=vmem(4),
        out_specs=vmem(1)[0],
        compiler_params=PARAMS,
        name="place",
    )(*base, place, back)
    return values, grad_down[None], grad_up[None]


def solution(mesh):
    return jax.shard_map(
        body,
        mesh=mesh,
        in_specs=(
            P(("fsdp", "dp"), None),
            P(("fsdp", "dp"), None),
            P(),
            P(("fsdp", "dp"), None),
            P(),
            P("fsdp", None, None),
            P("fsdp", None, None),
            P(("fsdp", "dp"), None),
        ),
        out_specs=(P(("fsdp", "dp"), None), P("fsdp", "dp", None), P("fsdp", None, "dp")),
        check_vma=False,
    )
```

time: 327 us -> 342 us (1.046)
  waiting for transfers between devices: 226 us -> 247 us
  Pallas kernels: 0 us -> 12.2 us
  matrix products: 17.7 us -> 5.84 us
  local copies, waits for them, and re-layouts: 19.6 us -> 12.8 us
  starting transfers between devices: 44.3 us -> 48 us
    all_gather x1 -> x2, waiting for transfers between devices: 95.7 us -> 162 us  [body(): lax.all_gather(frozen_value_weight[:, h * half:(h + 1) * half], ('fsdp',...]
    unnamed x4 -> x2, waiting for transfers between devices: 31.8 us -> 0.71 us
    reshape x6 -> x0, local copies, waits for them, and re-layouts: 16.5 us -> none  [the longest x1 7.46 us: body(): arrived_rows = arrived.reshape(-1, model_width)]
    all_to_all x3, waiting for transfers between devices: 98.7 us -> 84.6 us  [the longest x1 75.4 us: body(): lax.all_to_all(sent.reshape(fsdp, Q, columns), 'fsdp', split_axis=0, conc...]
    pallas_call x0 -> x4, Pallas kernels: none -> 12.2 us  [the longest x1 5.77 us: body(): pl.pallas_call(dispatch_kernel, out_shape=(jax.ShapeDtypeStruct((rows, co...]
    dot_general x7 -> x2, matrix products: 16.8 us -> 5.84 us  [body(): jnp.dot(tokens, weights[h], preferred_element_type=F32)]
    unnamed x9 -> x30, local copies, waits for them, and re-layouts: 1.48 us -> 10.8 us
    all_to_all x3, starting transfers between devices: 44.1 us -> 48 us  [the longest x1 19.7 us: body(): lax.all_to_all(sent.reshape(fsdp, Q, columns), 'fsdp', split_axis=0, conc...]
  transfers between devices with their start and end apart: 6 -> 5, of which waited for: 4 -> 4; matrix products, arithmetic and copies ran while one was open for 7% -> 2% of each run, Pallas kernels for 0% -> 4%
where the time goes in v1:
time: 342 us; the launch traced here: 341 us
  waiting for transfers between devices  247 us (72%)
  starting transfers between devices  48 us (14%)
  between operations  14.2 us (4%)
  local copies, waits for them, and re-layouts  12.8 us (4%)
  Pallas kernels  12.2 us (4%)
  matrix products  5.84 us (2%)
    all_gather x2, waiting for transfers between devices, body(): lax.all_gather(frozen_value_weight[:, h * half:(h + 1) * half], ('fsdp',...  162 us
    all_to_all x1, waiting for transfers between devices, body(): lax.all_to_all(sent.reshape(fsdp, Q, columns), 'fsdp', split_axis=0, conc...  75.4 us
    all_to_all x1, starting transfers between devices, body(): lax.all_to_all(sent.reshape(fsdp, Q, columns), 'fsdp', split_axis=0, conc...  19.7 us
    all_to_all x1, starting transfers between devices, body(): lax.all_to_all(grads.reshape(dp, rank, chunk + 2 * rank), 'dp', split_axi...  14.8 us
    all_to_all x1, starting transfers between devices, body(): lax.all_to_all(back.reshape(fsdp, Q, half), 'fsdp', split_axis=0, concat_...  13.4 us
    unnamed x30, local copies, waits for them, and re-layouts  10.8 us
    all_to_all x1, waiting for transfers between devices, body(): lax.all_to_all(back.reshape(fsdp, Q, half), 'fsdp', split_axis=0, concat_...  9.25 us
  transfers between devices with their start and end apart: 5, of which 4 were waited for; matrix products, arithmetic and copies ran while one was open for 2% of the time, Pallas kernels for 4%

profile of v1, /device:TPU:1, one launch (start us, length us, event | category | flops | bytes accessed | tf_op | source)
XLA Modules:
  0.0 340.9 jit_solution(296856627610228841)
XLA Ops:
  7.2 0.0 all-gather.5.cloned.1.call-start
  7.2 1.3 fusion.1
  8.5 0.0 all-gather.5.cloned.1.call-update
  8.6 0.0 copy-start
  8.6 1.6 copy-done
  10.1 0.0 copy-start.9
  10.1 0.9 copy-done.9
  11.1 0.0 copy-start.12
  11.1 0.7 copy-done.12
  11.7 0.0 copy-start.13
  11.7 0.7 copy-done.13
  12.4 5.8 %dispatch.1 = (bf16[512,3328]{1,0:T(8,128)(2,1)S(1)}, bf16[2,512,128]{2,1,0:T(8,128)(2,1)S(1)}) custom-call(s32[64]{0:T(128)S(1)} %copy-done.12, s32[1,128]{1,0:T(1,128)S(1)} %bitcast.28, bf16[128,8192]{1,0:T(8,128)(2,1)S(1)} %copy-done, bf16[128,512]{1,0:T(8,128)(2,1)S(1)} %copy-done.9), custom_call_target="tpu_custom_call" | custom-call | tf_op jit(solution)/shard_map/dispatch/pallas_call | solution.py:190
  18.1 0.0 copy-start.3
  18.1 1.7 copy-done.3
  19.9 0.0 copy-start.6
  19.9 0.7 copy-done.6
  20.6 19.7 %all-to-all-start = ((bf16[64,8,3328]{2,1,0:T(8,128)(2,1)}), bf16[64,8,3328]{2,1,0:T(8,128)(2,1)S(1)}, u32[]{:S(2)}, u32[]{:S(2)}) async-start(bf16[64,8,3328]{2,1,0:T(8,128)(2,1)} %bitcast.23), calls=%async_computation | async-start | bytes 6815744 | tf_op jit(solution)/shard_map/all_to_all | solution.py:202
  40.3 0.0 all-gather.3.cloned.1.call-start
  40.3 0.7 all-gather.3.cloned.1.call-update
  41.0 75.4 %all-to-all-done = bf16[64,8,3328]{2,1,0:T(8,128)(2,1)S(1)} async-done(((bf16[64,8,3328]{2,1,0:T(8,128)(2,1)}), bf16[64,8,3328]{2,1,0:T(8,128)(2,1)S(1)}, u32[]{:S(2)}, u32[]{:S(2)}) %all-to-all-start) | async-done | bytes 3407904 | tf_op jit(solution)/shard_map/all_to_all | solution.py:202
  116.4 0.0 copy-done.5
  116.4 0.0 copy-start.4
  116.4 1.2 copy-done.4
  117.6 2.2 correct.1
  119.8 0.0 copy-start.8
  119.9 0.7 copy-done.8
  120.6 0.0 copy-start.10
  120.6 0.7 copy-done.10
  121.2 13.4 %all-to-all-start.1 = ((bf16[64,8,256]{2,1,0:T(8,128)(2,1)}), bf16[64,8,256]{2,1,0:T(8,128)(2,1)}, u32[]{:S(2)}, u32[]{:S(2)}) async-start(bf16[64,8,256]{2,1,0:T(8,128)(2,1)} %bitcast.27), calls=%async_computation.1 | async-start | bytes 524288 | tf_op jit(solution)/shard_map/all_to_all | solution.py:218
  134.6 0.0 copy-start.11
  134.7 0.9 copy-done.11
  135.5 2.3 grads.1
  137.9 0.0 copy-start.2
  137.9 1.1 copy-done.2
  139.0 9.2 %all-to-all-done.1 = bf16[64,8,256]{2,1,0:T(8,128)(2,1)} async-done(((bf16[64,8,256]{2,1,0:T(8,128)(2,1)}), bf16[64,8,256]{2,1,0:T(8,128)(2,1)}, u32[]{:S(2)}, u32[]{:S(2)}) %all-to-all-start.1) | async-done | bytes 262176 | tf_op jit(solution)/shard_map/all_to_all | solution.py:218
  148.2 14.8 %all-to-all-start.2 = ((bf16[8,64,1152]{2,1,0:T(8,128)(2,1)}), bf16[8,64,1152]{2,1,0:T(8,128)(2,1)S(1)}, u32[]{:S(2)}, u32[]{:S(2)}) async-start(bf16[8,64,1152]{2,1,0:T(8,128)(2,1)} %bitcast.22), calls=%async_computation.2 | async-start | bytes 2359296 | tf_op jit(solution)/shard_map/all_to_all | solution.py:229
  163.0 0.0 copy-done.14
  163.1 48.2 %all-gather.5.cloned.1.call-done = bf16[8192,256]{1,0:T(8,128)(2,1)} async-done(((bf16[16,256]{1,0:T(8,128)(2,1)}), bf16[8192,256]{1,0:T(8,128)(2,1)}) %all-gather.5.cloned.1.call-update) | async-done | bytes 4194320 | tf_op jit(solution)/shard_map/all_gather | solution.py:183
  211.3 0.0 copy-done.1
  211.3 2.9 convolution_add_fusion.base1_ref
  214.2 113.5 %all-gather.3.cloned.1.call-done = bf16[8192,256]{1,0:T(8,128)(2,1)} async-done(((bf16[16,256]{1,0:T(8,128)(2,1)}), bf16[8192,256]{1,0:T(8,128)(2,1)}) %all-gather.3.cloned.1.call-update) | async-done | bytes 4194320 | tf_op jit(solution)/shard_map/all_gather | solution.py:183
  327.7 2.9 convolution_add_fusion.1.base0_ref
  330.6 0.0 copy-done.7
  330.6 1.9 place.1
  332.5 0.0 all-to-all-done.2
  332.5 0.2 convert_reduce_fusion
  332.7 0.7 slice_bitcast_fusion
  333.4 0.7 fusion
  (5 shorter events, 0.0 us)
Async XLA Ops:
  7.2 204.1 %all-gather.5.cloned.1.call-start = ((), (), s32[]{:S(2)}) async-start(), calls=%async_computation.4 | async-start | bytes 4202496 | tf_op jit(solution)/shard_map/all_gather | solution.py:183
  8.6 1.6 copy-start
  10.1 0.9 copy-start.9
  11.1 0.7 copy-start.12
  11.7 0.7 copy-start.13
  18.1 1.7 copy-start.3
  19.9 0.7 copy-start.6
  20.6 95.8 %copy-start.5 = (bf16[1,64,512]{2,1,0:T(8,128)(2,1)S(1)}, bf16[1,64,512]{2,1,0:T(8,128)(2,1)}, u32[]{:S(2)}) copy-start(bf16[1,64,512]{2,1,0:T(8,128)(2,1)} %param.14) | copy-start | bytes 196612
  20.6 95.8 %all-to-all-start = ((bf16[64,8,3328]{2,1,0:T(8,128)(2,1)}), bf16[64,8,3328]{2,1,0:T(8,128)(2,1)S(1)}, u32[]{:S(2)}, u32[]{:S(2)}) async-start(bf16[64,8,3328]{2,1,0:T(8,128)(2,1)} %bitcast.23), calls=%async_computation | async-start | bytes 6815744 | tf_op jit(solution)/shard_map/all_to_all | solution.py:202
  40.3 287.4 %all-gather.3.cloned.1.call-start = ((), (), s32[]{:S(2)}) async-start(), calls=%async_computation.3 | async-start | bytes 4202496 | tf_op jit(solution)/shard_map/all_gather | solution.py:183
  116.4 1.2 copy-start.4
  119.8 0.7 copy-start.8
  120.6 0.7 copy-start.10
  121.2 27.0 %all-to-all-start.1 = ((bf16[64,8,256]{2,1,0:T(8,128)(2,1)}), bf16[64,8,256]{2,1,0:T(8,128)(2,1)}, u32[]{:S(2)}, u32[]{:S(2)}) async-start(bf16[64,8,256]{2,1,0:T(8,128)(2,1)} %bitcast.27), calls=%async_computation.1 | async-start | bytes 524288 | tf_op jit(solution)/shard_map/all_to_all | solution.py:218
  134.6 0.9 copy-start.11
  137.9 1.1 copy-start.2
  139.0 24.1 %copy-start.14 = (bf16[512]{0:T(512)(128)(2,1)S(1)}, bf16[512]{0:T(512)(128)(2,1)}, u32[]{:S(2)}) copy-start(bf16[512]{0:T(512)(128)(2,1)} %param.12) | copy-start | bytes 3076
  139.0 72.3 %copy-start.1 = (bf16[128,8192]{1,0:T(8,128)(2,1)S(1)}, bf16[128,8192]{1,0:T(8,128)(2,1)}, u32[]{:S(2)}) copy-start(bf16[128,8192]{1,0:T(8,128)(2,1)} %tokens_ref.1) | copy-start | bytes 6291460
  148.2 184.3 %all-to-all-start.2 = ((bf16[8,64,1152]{2,1,0:T(8,128)(2,1)}), bf16[8,64,1152]{2,1,0:T(8,128)(2,1)S(1)}, u32[]{:S(2)}, u32[]{:S(2)}) async-start(bf16[8,64,1152]{2,1,0:T(8,128)(2,1)} %bitcast.22), calls=%async_computation.2 | async-start | bytes 2359296 | tf_op jit(solution)/shard_map/all_to_all | solution.py:229
  327.7 3.0 copy-start.7
Sparse Core Ops, SparseCore 0:
  12.7 198.4 all-gather.4
  215.4 112.1 all-gather.2

commit v2 on v1

--- a/solution.py
+++ b/solution.py
@@ -1,12 +1,19 @@
+import functools
+
 import jax
 import jax.numpy as jnp
 from jax import lax
 from jax.experimental import pallas as pl
 from jax.experimental.pallas import tpu as pltpu
+from jax.sharding import Mesh
 from jax.sharding import PartitionSpec as P
+
 
 SLOTS = 3
 Q = 8
+FSDP = ("x", "z", "yh")
+DP = ("yl", "core")
+PLANE = ("z", "yh", "yl")
 F32 = jnp.float32
 BF16 = jnp.bfloat16
 
@@ -143,11 +150,41 @@
         ]
 
 
-def place_kernel(base0_ref, base1_ref, place_ref, back_ref, values_ref):
+def base_kernel(count_x, where_ref, tokens_ref, bias_ref, gate_ref, *refs):
+    own, other, base_ref = refs[:count_x], refs[count_x : 2 * count_x], refs[-1]
+    groups, block, out_width = own[0].shape
+    depth = 2 * groups * block
+    first = where_ref[1] == 0
+    step = 16
+    rows = 2 * step * block
+    base_ref[...] = jnp.broadcast_to(bias_ref[...].astype(F32), base_ref.shape)
+    for k in range(count_x):
+        start = lax.rem(where_ref[0] + count_x - k, count_x) * depth
+
+        @pl.loop(0, groups // step)
+        def _(i):
+            mine = own[k][pl.ds(i * step, step)]
+            theirs = other[k][pl.ds(i * step, step)]
+            low = jnp.where(first, mine, theirs)
+            high = jnp.where(first, theirs, mine)
+            weight = jnp.concatenate(
+                [low.reshape(step, 1, block, out_width), high.reshape(step, 1, block, out_width)],
+                axis=1,
+            ).reshape(rows, out_width)
+            columns = pl.ds(pl.multiple_of(start + i * rows, rows), rows)
+            base_ref[...] += nn(tokens_ref[:, columns], weight)
+
+
+def gate_kernel(*refs):
+    refs[-1][...] = jnp.zeros_like(refs[-1])
+
+
+def place_kernel(base_ref, place_ref, back_ref, values_ref):
     half = back_ref.shape[1]
-    for h, base_ref in enumerate((base0_ref, base1_ref)):
+    for h in range(2):
         placed = tn(place_ref[h], back_ref[...])
-        values_ref[:, h * half : (h + 1) * half] = (base_ref[...] + placed).astype(BF16)
+        columns = slice(h * half, (h + 1) * half)
+        values_ref[:, columns] = (base_ref[:, columns] + placed).astype(BF16)
 
 
 def vmem(number):
@@ -169,24 +206,23 @@
 ):
     count, width = tokens.shape
     out_width = frozen_value_weight.shape[1]
-    fsdp = lax.axis_size("fsdp")
-    dp = lax.axis_size("dp")
+    fsdp = lax.axis_size(FSDP)
+    dp = lax.axis_size(DP)
+    size_x = lax.axis_size("x")
     rank = adapter_up_weight.shape[1]
     half = out_width // 2
     chunk = width // Q
     rows = fsdp * Q
     columns = SLOTS * chunk + half
 
-    weights = []
-    for h in range(2):
-        weights.append(
-            lax.all_gather(
-                frozen_value_weight[:, h * half : (h + 1) * half],
-                ("fsdp", "dp"),
-                axis=0,
-                tiled=True,
-            )
-        )
+    plane = lax.axis_size(PLANE)
+    piece = lax.all_to_all(
+        jnp.broadcast_to(frozen_value_weight[None], (plane, *frozen_value_weight.shape)),
+        PLANE,
+        split_axis=0,
+        concat_axis=0,
+        tiled=True,
+    )
     sent, place = pl.pallas_call(
         dispatch_kernel,
         out_shape=(
@@ -199,8 +235,23 @@
         compiler_params=PARAMS,
         name="dispatch",
     )(adapter_storage_index, token_adapter_index.reshape(1, count), tokens, cotangent)
+    sent, piece = lax.optimization_barrier((sent, piece))
+    own = [piece]
+    for k in range(1, size_x):
+        shift = [(i, (i + k) % size_x) for i in range(size_x)]
+        own.append(lax.ppermute(piece, "x", shift))
+    other = []
+    for k in range(size_x):
+        other.append(lax.ppermute(own[k], "core", [(0, 1), (1, 0)]))
+    gate = pl.pallas_call(
+        gate_kernel,
+        out_shape=jax.ShapeDtypeStruct((8, 128), F32),
+        in_specs=[pl.BlockSpec(memory_space=pl.ANY)] * size_x,
+        out_specs=vmem(1)[0],
+        name="gate",
+    )(*own[1:], other[0])
     arrived = lax.all_to_all(
-        sent.reshape(fsdp, Q, columns), "fsdp", split_axis=0, concat_axis=0, tiled=True
+        sent.reshape(fsdp, Q, columns), FSDP, split_axis=0, concat_axis=0, tiled=True
     ).reshape(rows, columns)
     down = jnp.swapaxes(adapter_down_weight[0], 0, 1)
     up = adapter_up_weight[0]
@@ -216,7 +267,7 @@
         name="correct",
     )(arrived, down, up)
     back = lax.all_to_all(
-        back.reshape(fsdp, Q, half), "fsdp", split_axis=0, concat_axis=0, tiled=True
+        back.reshape(fsdp, Q, half), FSDP, split_axis=0, concat_axis=0, tiled=True
     ).reshape(rows, half)
     grads = pl.pallas_call(
         grads_kernel,
@@ -228,45 +279,51 @@
     )(arrived, up, low)
     grads = lax.all_to_all(
         grads.reshape(dp, rank, chunk + 2 * rank),
-        "dp",
+        DP,
         split_axis=0,
         concat_axis=0,
         tiled=True,
     )
     grads = jnp.sum(grads.astype(F32), axis=0)
-    odd = lax.axis_index("dp") % 2 == 1
+    odd = lax.axis_index("core") == 1
     grad_up = jnp.where(odd, grads[:, chunk + rank :], grads[:, chunk : chunk + rank])
     grad_down = jnp.swapaxes(grads[:, :chunk], 0, 1)
-    base = [
-        jnp.dot(tokens, weights[h], preferred_element_type=F32)
-        + frozen_value_bias[h * half : (h + 1) * half].astype(F32)
-        for h in range(2)
-    ]
+    where = jnp.stack([lax.axis_index("x"), lax.axis_index("core")]).astype(jnp.int32)
+    base = pl.pallas_call(
+        functools.partial(base_kernel, size_x),
+        out_shape=jax.ShapeDtypeStruct((count, out_width), F32),
+        in_specs=[pl.BlockSpec(memory_space=pltpu.SMEM)] + vmem(3 + 2 * size_x),
+        out_specs=vmem(1)[0],
+        compiler_params=PARAMS,
+        name="base",
+    )(where, tokens, frozen_value_bias.reshape(1, out_width), gate, *own, *other)
     values = pl.pallas_call(
         place_kernel,
         out_shape=jax.ShapeDtypeStruct((count, out_width), BF16),
-        in_specs=vmem(4),
+        in_specs=vmem(3),
         out_specs=vmem(1)[0],
         compiler_params=PARAMS,
         name="place",
-    )(*base, place, back)
+    )(base, place, back)
     return values, grad_down[None], grad_up[None]
 
 
 def solution(mesh):
+    fine = Mesh(mesh.devices.reshape(4, 8, 2, 4, 2), FSDP + DP)
+    all_axes = FSDP + DP
     return jax.shard_map(
         body,
-        mesh=mesh,
+        mesh=fine,
         in_specs=(
-            P(("fsdp", "dp"), None),
-            P(("fsdp", "dp"), None),
+            P(all_axes, None),
+            P(all_axes, None),
             P(),
-            P(("fsdp", "dp"), None),
+            P(all_axes, None),
             P(),
-            P("fsdp", None, None),
-            P("fsdp", None, None),
-            P(("fsdp", "dp"), None),
+            P(FSDP, None, None),
+            P(FSDP, None, None),
+            P(all_axes, None),
         ),
-        out_specs=(P(("fsdp", "dp"), None), P("fsdp", "dp", None), P("fsdp", None, "dp")),
+        out_specs=(P(all_axes, None), P(FSDP, DP, None), P(FSDP, None, DP)),
         check_vma=False,
     )

time: 342 us -> 228 us (0.67)
  waiting for transfers between devices: 247 us -> 24.5 us
  blocking collectives: 0 us -> 85.3 us
  starting transfers between devices: 48 us -> 82 us
  between operations: 14.2 us -> 0.89 us
  Pallas kernels: 12.2 us -> 20 us
  matrix products: 5.84 us -> 0 us
    all_gather x2 -> x0, waiting for transfers between devices: 162 us -> none  [body(): lax.all_gather(frozen_value_weight[:, h * half:(h + 1) * half], ('fsdp',...]
    all_to_all x0 -> x1, blocking collectives: none -> 85.3 us  [body(): lax.all_to_all(sent.reshape(fsdp, Q, columns), FSDP, split_axis=0, concat...]
    all_to_all x3, waiting for transfers between devices: 84.6 us -> 19.2 us  [the longest x1 19.2 us: body(): lax.all_to_all(jnp.broadcast_to(frozen_value_weight[None], (plane, *froze...]
    ppermute x0 -> x7, starting transfers between devices: none -> 42 us  [the longest x4 32.8 us: body(): other.append(lax.ppermute(own[k], 'core', [(0, 1), (1, 0)]))]
    all_to_all x3, starting transfers between devices: 48 us -> 40 us  [the longest x1 17.1 us: body(): lax.all_to_all(jnp.broadcast_to(frozen_value_weight[None], (plane, *froze...]
    pallas_call x0 -> x2, Pallas kernels: none -> 7.86 us  [the longest x1 7.27 us: body(): pl.pallas_call(functools.partial(base_kernel, size_x), out_shape=jax.Shap...]
    dot_general x2 -> x0, matrix products: 5.84 us -> none  [body(): jnp.dot(tokens, weights[h], preferred_element_type=F32)]
    ppermute x0 -> x7, waiting for transfers between devices: none -> 5.24 us  [the longest x3 4.38 us: body(): own.append(lax.ppermute(piece, 'x', shift))]
  transfers between devices with their start and end apart: 5 -> 10, of which waited for: 4 -> 4; matrix products, arithmetic and copies ran while one was open for 2% -> 0% of each run, Pallas kernels for 4% -> 8%
where the time goes in v2:
time: 228 us; the launch traced here: 226 us
  blocking collectives  85.3 us (37%)
  starting transfers between devices  82 us (36%)
  waiting for transfers between devices  24.5 us (11%)
  Pallas kernels  20 us (9%)
  local copies, waits for them, and re-layouts  12.4 us (5%)
    all_to_all x1, blocking collectives, body(): lax.all_to_all(sent.reshape(fsdp, Q, columns), FSDP, split_axis=0, concat...  85.3 us
    ppermute x4, starting transfers between devices, body(): other.append(lax.ppermute(own[k], 'core', [(0, 1), (1, 0)]))  32.8 us
    all_to_all x1, waiting for transfers between devices, body(): lax.all_to_all(jnp.broadcast_to(frozen_value_weight[None], (plane, *froze...  19.2 us
    all_to_all x1, starting transfers between devices, body(): lax.all_to_all(jnp.broadcast_to(frozen_value_weight[None], (plane, *froze...  17.1 us
    all_to_all x1, starting transfers between devices, body(): lax.all_to_all(back.reshape(fsdp, Q, half), FSDP, split_axis=0, concat_ax...  14.4 us
    unnamed x38, local copies, waits for them, and re-layouts  9.72 us
    ppermute x3, starting transfers between devices, body(): own.append(lax.ppermute(piece, 'x', shift))  9.13 us
    all_to_all x1, starting transfers between devices, body(): lax.all_to_all(grads.reshape(dp, rank, chunk + 2 * rank), DP, split_axis=...  8.52 us
  transfers between devices with their start and end apart: 10, of which 4 were waited for; matrix products, arithmetic and copies ran while one was open for 0% of the time, Pallas kernels for 8%

profile of v2, /device:TPU:1, one launch (start us, length us, event | category | flops | bytes accessed | tf_op | source)
XLA Modules:
  0.0 226.0 jit_solution(11880328011871426073)
XLA Ops:
  0.6 0.0 copy-start
  0.6 0.0 copy-start.12
  0.7 0.0 copy-start.16
  0.7 0.0 copy-start.17
  0.7 2.0 broadcast_in_dim.12
  2.7 17.1 %all-to-all-start = ((bf16[64,16,512]{2,1,0:T(8,128)(2,1)}), bf16[64,16,512]{2,1,0:T(8,128)(2,1)S(1)}, u32[]{:S(2)}, u32[]{:S(2)}) async-start(bf16[64,16,512]{2,1,0:T(8,128)(2,1)} %broadcast_in_dim.12), calls=%async_computation | async-start | bytes 2097152 | tf_op jit(solution)/shard_map/all_to_all | solution.py:219
  19.8 0.0 copy-done
  19.8 5.8 %dispatch.1 = (bf16[512,3328]{1,0:T(8,128)(2,1)S(1)}, bf16[2,512,128]{2,1,0:T(8,128)(2,1)S(1)}) custom-call(s32[64]{0:T(128)S(1)} %copy-done.16, s32[1,128]{1,0:T(1,128)S(1)} %bitcast.26, bf16[128,8192]{1,0:T(8,128)(2,1)S(1)} %copy-done, bf16[128,512]{1,0:T(8,128)(2,1)S(1)} %copy-done.12), custom_call_target="tpu_custom_call" | custom-call | tf_op jit(solution)/shard_map/dispatch/pallas_call | solution.py:226
  25.6 1.8 copy-done.6
  27.4 0.7 copy-done.9
  28.1 19.2 %all-to-all-done.refs_0_ = bf16[64,16,512]{2,1,0:T(8,128)(2,1)S(1)} async-done(((bf16[64,16,512]{2,1,0:T(8,128)(2,1)}), bf16[64,16,512]{2,1,0:T(8,128)(2,1)S(1)}, u32[]{:S(2)}, u32[]{:S(2)}) %all-to-all-start) | async-done | bytes 1048608 | tf_op jit(solution)/shard_map/all_to_all | solution.py:219
  47.3 1.0 copy-done.4
  48.2 85.3 %all_to_all.20 = bf16[64,8,3328]{2,1,0:T(8,128)(2,1)S(1)} all-to-all(bf16[64,8,3328]{2,1,0:T(8,128)(2,1)} %bitcast.21), channel_id=1, replica_groups=mesh['x'=4,'z'=8,'yh'=2,'yl'=4,'core'=2] {'x','z','yh'}, dimensions={0} | all-to-all | bytes 6815744 | tf_op jit(solution)/shard_map/all_to_all | solution.py:253
  133.6 2.2 correct.1
  135.8 0.7 copy-done.11
  136.5 0.7 copy-done.13
  137.1 14.4 %all-to-all-start.2 = ((bf16[64,8,256]{2,1,0:T(8,128)(2,1)}), bf16[64,8,256]{2,1,0:T(8,128)(2,1)}, u32[]{:S(2)}, u32[]{:S(2)}) async-start(bf16[64,8,256]{2,1,0:T(8,128)(2,1)} %bitcast.25), calls=%async_computation.2 | async-start | bytes 524288 | tf_op jit(solution)/shard_map/all_to_all | solution.py:269
  151.5 4.3 %collective-permute-start.2 = (bf16[64,16,512]{2,1,0:T(8,128)(2,1)}, bf16[64,16,512]{2,1,0:T(8,128)(2,1)}, u32[]{:S(2)}, u32[]{:S(2)}) collective-permute-start(bf16[64,16,512]{2,1,0:T(8,128)(2,1)} %copy-done.4), channel_id=1, source_target_pairs={{0,384},{128,0},{256,128},{384,256},{1,385},{129,1},{257,129},{385... | collective-permute-start | bytes 3145736 | tf_op jit(solution)/shard_map/ppermute | solution.py:242
  155.8 2.3 %collective-permute-start.1 = (bf16[64,16,512]{2,1,0:T(8,128)(2,1)}, bf16[64,16,512]{2,1,0:T(8,128)(2,1)}, u32[]{:S(2)}, u32[]{:S(2)}) collective-permute-start(bf16[64,16,512]{2,1,0:T(8,128)(2,1)} %copy-done.4), channel_id=1, source_target_pairs={{0,256},{128,384},{256,0},{384,128},{1,257},{129,385},{257,1},{385... | collective-permute-start | bytes 3145736 | tf_op jit(solution)/shard_map/ppermute | solution.py:242
  158.1 2.6 %collective-permute-start = (bf16[64,16,512]{2,1,0:T(8,128)(2,1)}, bf16[64,16,512]{2,1,0:T(8,128)(2,1)}, u32[]{:S(2)}, u32[]{:S(2)}) collective-permute-start(bf16[64,16,512]{2,1,0:T(8,128)(2,1)} %copy-done.4), channel_id=1, source_target_pairs={{0,128},{128,256},{256,384},{384,0},{1,129},{129,257},{257,385},{3... | collective-permute-start | bytes 3145736 | tf_op jit(solution)/shard_map/ppermute | solution.py:242
  160.7 0.0 copy-start.14
  160.7 0.9 copy-done.14
  161.6 2.3 %grads.1 = bf16[512,1152]{1,0:T(8,128)(2,1)S(1)} custom-call(bf16[512,3328]{1,0:T(8,128)(2,1)S(1)} %bitcast.19, bf16[64,512]{1,0:T(8,128)(2,1)S(1)} %bitcast.24, bf16[512,128]{1,0:T(8,128)(2,1)S(1)} %copy-done.14), custom_call_target="tpu_custom_call" | custom-call | tf_op jit(solution)/shard_map/grads/pallas_call | solution.py:272
  163.9 1.0 copy-done.1
  165.0 0.0 all-to-all-done.2
  165.0 8.5 %all-to-all-start.3 = ((bf16[8,64,1152]{2,1,0:T(8,128)(2,1)}), bf16[8,64,1152]{2,1,0:T(8,128)(2,1)S(1)}, u32[]{:S(2)}, u32[]{:S(2)}) async-start(bf16[8,64,1152]{2,1,0:T(8,128)(2,1)} %bitcast.20), calls=%async_computation.3 | async-start | bytes 2359296 | tf_op jit(solution)/shard_map/all_to_all | solution.py:280
  173.5 1.9 collective-permute-start.3
  175.5 3.8 %collective-permute-done.2.refs_2_.refs_3_ = bf16[64,16,512]{2,1,0:T(8,128)(2,1)} collective-permute-done((bf16[64,16,512]{2,1,0:T(8,128)(2,1)}, bf16[64,16,512]{2,1,0:T(8,128)(2,1)}, u32[]{:S(2)}, u32[]{:S(2)}) %collective-permute-start.2) | collective-permute-done | bytes 1048608 | tf_op jit(solution)/shard_map/ppermute | solution.py:242
  179.3 26.6 %collective-permute-start.6 = (bf16[64,16,512]{2,1,0:T(8,128)(2,1)}, bf16[64,16,512]{2,1,0:T(8,128)(2,1)}, u32[]{:S(2)}, u32[]{:S(2)}) collective-permute-start(bf16[64,16,512]{2,1,0:T(8,128)(2,1)} %collective-permute-done.2.refs_2_.refs_3_), channel_id=1, source_target_pairs={{0,1},{1,0},{2,3},{3,2},{4,5},{5,4},{6,7},{7,6},{8,9},{9,8},{10,11... | collective-permute-start | bytes 3145736 | tf_op jit(solution)/shard_map/ppermute | solution.py:245
  205.9 0.0 collective-permute-done.1.refs_1_.refs_2_
  205.9 1.9 collective-permute-start.5
  207.8 0.5 collective-permute-done.refs_0_.refs_1_
  208.4 2.4 %collective-permute-start.4 = (bf16[64,16,512]{2,1,0:T(8,128)(2,1)}, bf16[64,16,512]{2,1,0:T(8,128)(2,1)}, u32[]{:S(2)}, u32[]{:S(2)}) collective-permute-start(bf16[64,16,512]{2,1,0:T(8,128)(2,1)} %collective-permute-done.refs_0_.refs_1_), channel_id=1, source_target_pairs={{0,1},{1,0},{2,3},{3,2},{4,5},{5,4},{6,7},{7,6},{8,9},{9,8},{10,11... | collective-permute-start | bytes 3145736 | tf_op jit(solution)/shard_map/ppermute | solution.py:245
  210.8 0.1 pad_add_fusion.where_ref
  210.9 0.0 collective-permute-done.3.refs_3_.refs_4_
  210.9 1.0 copy-done.2
  211.9 0.6 gate.1.gate_ref
  212.5 0.0 collective-permute-done.6.refs_7_
  212.5 0.0 collective-permute-done.5.refs_6_
  212.5 0.9 collective-permute-done.4.refs_5_
  213.4 1.2 copy-done.3
  214.6 0.7 copy-done.15
  215.3 7.3 %base.1.base_ref = f32[128,512]{1,0:T(8,128)S(1)} custom-call(s32[2]{0:T(128)S(1)} %pad_add_fusion.where_ref, bf16[128,8192]{1,0:T(8,128)(2,1)} %tokens_ref.3, bf16[1,512]{1,0:T(2,128)(2,1)S(1)} %reshape.28.bias_ref, f32[8,128]{1,0:T(8,128)S(1)} %copy-done.15, bf16[64,16,512]{2,1,0:T(8,128)(2,1)S(1)} %copy-done.5, ...), custom_call_target="tpu_custom_call" | custom-call | tf_op jit(solution)/shard_map/base/pallas_call | solution.py:292
  222.6 1.9 place.1
  224.5 0.0 all-to-all-done.3
  224.5 0.2 convert_reduce_fusion
  224.6 0.7 slice_bitcast_fusion
  225.4 0.7 fusion
  (23 shorter events, 0.0 us)
Async XLA Ops:
  0.6 19.2 %copy-start = (bf16[128,8192]{1,0:T(8,128)(2,1)S(1)}, bf16[128,8192]{1,0:T(8,128)(2,1)}, u32[]{:S(2)}) copy-start(bf16[128,8192]{1,0:T(8,128)(2,1)} %tokens_ref.3) | copy-start | bytes 6291460
  0.6 19.2 %copy-start.12 = (bf16[128,512]{1,0:T(8,128)(2,1)S(1)}, bf16[128,512]{1,0:T(8,128)(2,1)}, u32[]{:S(2)}) copy-start(bf16[128,512]{1,0:T(8,128)(2,1)} %cot_ref.1) | copy-start | bytes 393220
  0.7 19.2 %copy-start.16 = (s32[64]{0:T(128)S(1)}, s32[64]{0:T(128)}, u32[]{:S(2)}) copy-start(s32[64]{0:T(128)} %storage_ref.1) | copy-start | bytes 772
  0.7 19.2 %copy-start.17 = (s32[128,1]{0,1:T(1,128)S(1)}, s32[128,1]{0,1:T(1,128)}, u32[]{:S(2)}) copy-start(s32[128,1]{0,1:T(1,128)} %param.9) | copy-start | bytes 1540
  2.7 44.6 %all-to-all-start = ((bf16[64,16,512]{2,1,0:T(8,128)(2,1)}), bf16[64,16,512]{2,1,0:T(8,128)(2,1)S(1)}, u32[]{:S(2)}, u32[]{:S(2)}) async-start(bf16[64,16,512]{2,1,0:T(8,128)(2,1)} %broadcast_in_dim.12), calls=%async_computation | async-start | bytes 2097152 | tf_op jit(solution)/shard_map/all_to_all | solution.py:219
  25.6 1.8 copy-start.6
  27.4 0.7 copy-start.9
  47.3 1.0 copy-start.4
  48.2 85.3 %copy-start.7 = (bf16[1,8192,64]{1,2,0:T(8,128)(2,1)S(1)}, bf16[1,8192,64]{1,2,0:T(8,128)(2,1)}, u32[]{:S(2)}) copy-start(bf16[1,8192,64]{1,2,0:T(8,128)(2,1)} %param.13) | copy-start | bytes 3145732
  48.2 85.3 %copy-start.8 = (bf16[1,64,512]{2,1,0:T(8,128)(2,1)S(1)}, bf16[1,64,512]{2,1,0:T(8,128)(2,1)}, u32[]{:S(2)}) copy-start(bf16[1,64,512]{2,1,0:T(8,128)(2,1)} %param.14) | copy-start | bytes 196612
  135.8 0.7 copy-start.11
  136.5 0.7 copy-start.13
  137.1 27.9 %all-to-all-start.2 = ((bf16[64,8,256]{2,1,0:T(8,128)(2,1)}), bf16[64,8,256]{2,1,0:T(8,128)(2,1)}, u32[]{:S(2)}, u32[]{:S(2)}) async-start(bf16[64,8,256]{2,1,0:T(8,128)(2,1)} %bitcast.25), calls=%async_computation.2 | async-start | bytes 524288 | tf_op jit(solution)/shard_map/all_to_all | solution.py:269
  151.5 27.8 %collective-permute-start.2 = (bf16[64,16,512]{2,1,0:T(8,128)(2,1)}, bf16[64,16,512]{2,1,0:T(8,128)(2,1)}, u32[]{:S(2)}, u32[]{:S(2)}) collective-permute-start(bf16[64,16,512]{2,1,0:T(8,128)(2,1)} %copy-done.4), channel_id=1, source_target_pairs={{0,384},{128,0},{256,128},{384,256},{1,385},{129,1},{257,129},{385... | collective-permute-start | bytes 3145736 | tf_op jit(solution)/shard_map/ppermute | solution.py:242
  155.8 50.1 %collective-permute-start.1 = (bf16[64,16,512]{2,1,0:T(8,128)(2,1)}, bf16[64,16,512]{2,1,0:T(8,128)(2,1)}, u32[]{:S(2)}, u32[]{:S(2)}) collective-permute-start(bf16[64,16,512]{2,1,0:T(8,128)(2,1)} %copy-done.4), channel_id=1, source_target_pairs={{0,256},{128,384},{256,0},{384,128},{1,257},{129,385},{257,1},{385... | collective-permute-start | bytes 3145736 | tf_op jit(solution)/shard_map/ppermute | solution.py:242
  158.1 50.3 %collective-permute-start = (bf16[64,16,512]{2,1,0:T(8,128)(2,1)}, bf16[64,16,512]{2,1,0:T(8,128)(2,1)}, u32[]{:S(2)}, u32[]{:S(2)}) collective-permute-start(bf16[64,16,512]{2,1,0:T(8,128)(2,1)} %copy-done.4), channel_id=1, source_target_pairs={{0,128},{128,256},{256,384},{384,0},{1,129},{129,257},{257,385},{3... | collective-permute-start | bytes 3145736 | tf_op jit(solution)/shard_map/ppermute | solution.py:242
  160.7 0.9 copy-start.14
  163.9 1.0 copy-start.1
  165.0 8.6 %copy-start.5 = (bf16[64,16,512]{2,1,0:T(8,128)(2,1)S(1)}, bf16[64,16,512]{2,1,0:T(8,128)(2,1)}, u32[]{:S(2)}) copy-start(bf16[64,16,512]{2,1,0:T(8,128)(2,1)} %copy-done.4) | copy-start | bytes 3145732
  165.0 45.8 %copy-start.18 = (bf16[512]{0:T(512)(128)(2,1)S(1)}, bf16[512]{0:T(512)(128)(2,1)}, u32[]{:S(2)}) copy-start(bf16[512]{0:T(512)(128)(2,1)} %param.12) | copy-start | bytes 3076
  165.0 59.5 %all-to-all-start.3 = ((bf16[8,64,1152]{2,1,0:T(8,128)(2,1)}), bf16[8,64,1152]{2,1,0:T(8,128)(2,1)S(1)}, u32[]{:S(2)}, u32[]{:S(2)}) async-start(bf16[8,64,1152]{2,1,0:T(8,128)(2,1)} %bitcast.20), calls=%async_computation.3 | async-start | bytes 2359296 | tf_op jit(solution)/shard_map/all_to_all | solution.py:280
  173.5 37.4 %collective-permute-start.3 = (bf16[64,16,512]{2,1,0:T(8,128)(2,1)S(1)}, bf16[64,16,512]{2,1,0:T(8,128)(2,1)S(1)}, u32[]{:S(2)}, u32[]{:S(2)}) collective-permute-start(bf16[64,16,512]{2,1,0:T(8,128)(2,1)S(1)} %copy-done.5), channel_id=1, source_target_pairs={{0,1},{1,0},{2,3},{3,2},{4,5},{5,4},{6,7},{7,6},{8,9},{9,8},{10,11... | collective-permute-start | bytes 3145736 | tf_op jit(solution)/shard_map/ppermute | solution.py:245
  179.3 33.2 %collective-permute-start.6 = (bf16[64,16,512]{2,1,0:T(8,128)(2,1)}, bf16[64,16,512]{2,1,0:T(8,128)(2,1)}, u32[]{:S(2)}, u32[]{:S(2)}) collective-permute-start(bf16[64,16,512]{2,1,0:T(8,128)(2,1)} %collective-permute-done.2.refs_2_.refs_3_), channel_id=1, source_target_pairs={{0,1},{1,0},{2,3},{3,2},{4,5},{5,4},{6,7},{7,6},{8,9},{9,8},{10,11... | collective-permute-start | bytes 3145736 | tf_op jit(solution)/shard_map/ppermute | solution.py:245
  205.9 6.6 %collective-permute-start.5 = (bf16[64,16,512]{2,1,0:T(8,128)(2,1)}, bf16[64,16,512]{2,1,0:T(8,128)(2,1)}, u32[]{:S(2)}, u32[]{:S(2)}) collective-permute-start(bf16[64,16,512]{2,1,0:T(8,128)(2,1)} %collective-permute-done.1.refs_1_.refs_2_), channel_id=1, source_target_pairs={{0,1},{1,0},{2,3},{3,2},{4,5},{5,4},{6,7},{7,6},{8,9},{9,8},{10,11... | collective-permute-start | bytes 3145736 | tf_op jit(solution)/shard_map/ppermute | solution.py:245
  208.4 5.0 %collective-permute-start.4 = (bf16[64,16,512]{2,1,0:T(8,128)(2,1)}, bf16[64,16,512]{2,1,0:T(8,128)(2,1)}, u32[]{:S(2)}, u32[]{:S(2)}) collective-permute-start(bf16[64,16,512]{2,1,0:T(8,128)(2,1)} %collective-permute-done.refs_0_.refs_1_), channel_id=1, source_target_pairs={{0,1},{1,0},{2,3},{3,2},{4,5},{5,4},{6,7},{7,6},{8,9},{9,8},{10,11... | collective-permute-start | bytes 3145736 | tf_op jit(solution)/shard_map/ppermute | solution.py:245
  210.9 1.0 copy-start.2
  211.9 10.6 %copy-start.10 = (bf16[2,512,128]{2,1,0:T(8,128)(2,1)S(1)}, bf16[2,512,128]{2,1,0:T(8,128)(2,1)}, u32[]{:S(2)}) copy-start(bf16[2,512,128]{2,1,0:T(8,128)(2,1)} %copy-done.9) | copy-start | bytes 786436
  213.4 1.2 copy-start.3
  214.6 0.7 copy-start.15

commit v3 on v2

--- a/solution.py
+++ b/solution.py
@@ -13,7 +13,8 @@
 Q = 8
 FSDP = ("x", "z", "yh")
 DP = ("yl", "core")
-PLANE = ("z", "yh", "yl")
+COLUMN = ("yh", "yl")
+SWAP = ((0, 1), (1, 0))
 F32 = jnp.float32
 BF16 = jnp.bfloat16
 
@@ -114,7 +115,7 @@
     back_ref[...] = nn(low, stacked_up(up_ref)).astype(BF16)
 
 
-def grads_kernel(arrived_ref, up_ref, low_ref, grad_ref):
+def grads_kernel(where_ref, arrived_ref, up_ref, low_ref, keep_ref, give_ref, grad_ref):
     rows = arrived_ref.shape[0]
     rank = up_ref.shape[0]
     chunk = grad_ref.shape[1] - 2 * rank
@@ -139,8 +140,8 @@
             ],
             axis=0,
         )
-        grad_ref[:, start : start + step] = tn(left, right).astype(BF16)
-    up = tn(low_ref[...], cot).astype(BF16)
+        grad_ref[:, start : start + step] = tn(left, right)
+    up = tn(low_ref[...], cot)
     per_half = Q // 2
     for d in range(Q):
         column = (d % per_half) // 2 * 2 * rank
@@ -148,21 +149,54 @@
         grad_ref[d * rank : (d + 1) * rank, chunk:] = up[
             first : first + rank, column : column + 2 * rank
         ]
-
-
-def base_kernel(count_x, where_ref, tokens_ref, bias_ref, gate_ref, *refs):
-    own, other, base_ref = refs[:count_x], refs[count_x : 2 * count_x], refs[-1]
+    core = where_ref[3]
+    for y in range(Q // 2):
+        block = slice(y * rank, (y + 1) * rank)
+        keep_ref[block] = grad_ref[pl.ds(pl.multiple_of((2 * y + core) * rank, rank), rank)]
+        give_ref[block] = grad_ref[
+            pl.ds(pl.multiple_of((2 * y + 1 - core) * rank, rank), rank)
+        ].astype(BF16)
+
+
+def middle_kernel(where_ref, keep_ref, taken_ref, mine_ref, *sent_refs):
+    count = 1 + len(sent_refs)
+    rank = mine_ref.shape[0]
+    for k in range(count):
+        y = lax.rem(where_ref[2] + k, count)
+        rows = pl.ds(pl.multiple_of(y * rank, rank), rank)
+        total = keep_ref[rows] + taken_ref[rows].astype(F32)
+        if k == 0:
+            mine_ref[...] = total
+        else:
+            sent_refs[k - 1][...] = total.astype(BF16)
+
+
+def finish_kernel(where_ref, mine_ref, *refs):
+    taken, (down_ref, up_ref) = refs[:-2], refs[-2:]
+    rank = mine_ref.shape[0]
+    chunk = down_ref.shape[1]
+    total = mine_ref[...]
+    for ref in taken:
+        total = total + ref[...].astype(F32)
+    down_ref[...] = total[:, :chunk]
+    up_ref[...] = jnp.where(
+        where_ref[3] == 1, pltpu.roll(total[:, chunk:], rank, 1), total[:, chunk:]
+    )[:, :rank]
+
+
+def base_kernel(size_x, size_z, where_ref, tokens_ref, bias_ref, gate_ref, *refs):
+    own, other, base_ref = refs[:size_x], refs[size_x : 2 * size_x], refs[-1]
     groups, block, out_width = own[0].shape
-    depth = 2 * groups * block
-    first = where_ref[1] == 0
-    step = 16
+    step = groups // size_z
     rows = 2 * step * block
+    first = where_ref[3] == 0
     base_ref[...] = jnp.broadcast_to(bias_ref[...].astype(F32), base_ref.shape)
-    for k in range(count_x):
-        start = lax.rem(where_ref[0] + count_x - k, count_x) * depth
-
-        @pl.loop(0, groups // step)
+    for k in range(size_x):
+        from_x = lax.rem(where_ref[0] + size_x - k, size_x)
+
+        @pl.loop(0, size_z)
         def _(i):
+            from_z = lax.rem(where_ref[1] + size_z - i, size_z)
             mine = own[k][pl.ds(i * step, step)]
             theirs = other[k][pl.ds(i * step, step)]
             low = jnp.where(first, mine, theirs)
@@ -171,7 +205,7 @@
                 [low.reshape(step, 1, block, out_width), high.reshape(step, 1, block, out_width)],
                 axis=1,
             ).reshape(rows, out_width)
-            columns = pl.ds(pl.multiple_of(start + i * rows, rows), rows)
+            columns = pl.ds(pl.multiple_of((from_x * size_z + from_z) * rows, rows), rows)
             base_ref[...] += nn(tokens_ref[:, columns], weight)
 
 
@@ -209,20 +243,17 @@
     fsdp = lax.axis_size(FSDP)
     dp = lax.axis_size(DP)
     size_x = lax.axis_size("x")
+    size_z = lax.axis_size("z")
+    size_y = lax.axis_size("yl")
+    where = jnp.stack([lax.axis_index(n) for n in ("x", "z", "yl", "core")]).astype(jnp.int32)
+    smem = [pl.BlockSpec(memory_space=pltpu.SMEM)]
     rank = adapter_up_weight.shape[1]
     half = out_width // 2
     chunk = width // Q
     rows = fsdp * Q
     columns = SLOTS * chunk + half
 
-    plane = lax.axis_size(PLANE)
-    piece = lax.all_to_all(
-        jnp.broadcast_to(frozen_value_weight[None], (plane, *frozen_value_weight.shape)),
-        PLANE,
-        split_axis=0,
-        concat_axis=0,
-        tiled=True,
-    )
+    column = lax.all_gather(frozen_value_weight, COLUMN, axis=0, tiled=True)
     sent, place = pl.pallas_call(
         dispatch_kernel,
         out_shape=(
@@ -235,21 +266,26 @@
         compiler_params=PARAMS,
         name="dispatch",
     )(adapter_storage_index, token_adapter_index.reshape(1, count), tokens, cotangent)
-    sent, piece = lax.optimization_barrier((sent, piece))
+    sent, column = lax.optimization_barrier((sent, column))
+    parts = [column]
+    for k in range(1, size_z):
+        climb = [(i, (i + k) % size_z) for i in range(size_z)]
+        parts.append(lax.ppermute(column, "z", climb))
+    piece = jnp.concatenate(parts, axis=0).reshape(-1, *frozen_value_weight.shape)
     own = [piece]
     for k in range(1, size_x):
         shift = [(i, (i + k) % size_x) for i in range(size_x)]
         own.append(lax.ppermute(piece, "x", shift))
     other = []
     for k in range(size_x):
-        other.append(lax.ppermute(own[k], "core", [(0, 1), (1, 0)]))
+        other.append(lax.ppermute(own[k], "core", SWAP))
     gate = pl.pallas_call(
         gate_kernel,
         out_shape=jax.ShapeDtypeStruct((8, 128), F32),
-        in_specs=[pl.BlockSpec(memory_space=pl.ANY)] * size_x,
+        in_specs=[pl.BlockSpec(memory_space=pl.ANY)],
         out_specs=vmem(1)[0],
         name="gate",
-    )(*own[1:], other[0])
+    )(other[0])
     arrived = lax.all_to_all(
         sent.reshape(fsdp, Q, columns), FSDP, split_axis=0, concat_axis=0, tiled=True
     ).reshape(rows, columns)
@@ -269,30 +305,37 @@
     back = lax.all_to_all(
         back.reshape(fsdp, Q, half), FSDP, split_axis=0, concat_axis=0, tiled=True
     ).reshape(rows, half)
-    grads = pl.pallas_call(
+    wide = chunk + 2 * rank
+    keep, give = pl.pallas_call(
         grads_kernel,
-        out_shape=jax.ShapeDtypeStruct((dp * rank, chunk + 2 * rank), BF16),
-        in_specs=vmem(3),
-        out_specs=vmem(1)[0],
+        out_shape=(
+            jax.ShapeDtypeStruct((size_y * rank, wide), F32),
+            jax.ShapeDtypeStruct((size_y * rank, wide), BF16),
+        ),
+        in_specs=smem + vmem(3),
+        out_specs=tuple(vmem(2)),
+        scratch_shapes=[pltpu.VMEM((dp * rank, wide), F32)],
         compiler_params=PARAMS,
         name="grads",
-    )(arrived, up, low)
-    grads = lax.all_to_all(
-        grads.reshape(dp, rank, chunk + 2 * rank),
-        DP,
-        split_axis=0,
-        concat_axis=0,
-        tiled=True,
-    )
-    grads = jnp.sum(grads.astype(F32), axis=0)
-    odd = lax.axis_index("core") == 1
-    grad_up = jnp.where(odd, grads[:, chunk + rank :], grads[:, chunk : chunk + rank])
-    grad_down = jnp.swapaxes(grads[:, :chunk], 0, 1)
-    where = jnp.stack([lax.axis_index("x"), lax.axis_index("core")]).astype(jnp.int32)
+    )(where, arrived, up, low)
+    taken = lax.ppermute(give, "core", SWAP)
+    mine, *sums = pl.pallas_call(
+        middle_kernel,
+        out_shape=(jax.ShapeDtypeStruct((rank, wide), F32),)
+        + (jax.ShapeDtypeStruct((rank, wide), BF16),) * (size_y - 1),
+        in_specs=smem + vmem(2),
+        out_specs=tuple(vmem(size_y)),
+        compiler_params=PARAMS,
+        name="middle",
+    )(where, keep, taken)
+    arrivals = []
+    for k in range(1, size_y):
+        rise = [(i, (i + k) % size_y) for i in range(size_y)]
+        arrivals.append(lax.ppermute(sums[k - 1], "yl", rise))
     base = pl.pallas_call(
-        functools.partial(base_kernel, size_x),
+        functools.partial(base_kernel, size_x, size_z),
         out_shape=jax.ShapeDtypeStruct((count, out_width), F32),
-        in_specs=[pl.BlockSpec(memory_space=pltpu.SMEM)] + vmem(3 + 2 * size_x),
+        in_specs=smem + vmem(3 + 2 * size_x),
         out_specs=vmem(1)[0],
         compiler_params=PARAMS,
         name="base",
@@ -305,7 +348,18 @@
         compiler_params=PARAMS,
         name="place",
     )(base, place, back)
-    return values, grad_down[None], grad_up[None]
+    grad_down, grad_up = pl.pallas_call(
+        finish_kernel,
+        out_shape=(
+            jax.ShapeDtypeStruct((rank, chunk), F32),
+            jax.ShapeDtypeStruct((rank, rank), F32),
+        ),
+        in_specs=smem + vmem(size_y),
+        out_specs=tuple(vmem(2)),
+        compiler_params=PARAMS,
+        name="finish",
+    )(where, mine, *arrivals)
+    return values, jnp.swapaxes(grad_down, 0, 1)[None], grad_up[None]
 
 
 def solution(mesh):

time: 228 us -> 269 us (1.18)
  blocking collectives: 85.3 us -> 22.8 us
  waiting for transfers between devices: 24.5 us -> 71.6 us
  starting transfers between devices: 82 us -> 125 us
  Pallas kernels: 20 us -> 27.7 us
  local copies, waits for them, and re-layouts: 12.4 us -> 19.2 us
    all_to_all x1 -> x0, blocking collectives: 85.3 us -> none  [body(): lax.all_to_all(sent.reshape(fsdp, Q, columns), FSDP, split_axis=0, concat...]
    ppermute x4 -> x15, waiting for transfers between devices: 0.86 us -> 71.6 us  [the longest x7 71.6 us: body(): parts.append(lax.ppermute(column, 'z', climb))]
    ppermute x4 -> x15, starting transfers between devices: 32.8 us -> 80.8 us  [the longest x4 48.7 us: body(): other.append(lax.ppermute(own[k], 'core', SWAP))]
    all_gather x0 -> x1, blocking collectives: none -> 22.8 us  [body(): column = lax.all_gather(frozen_value_weight, COLUMN, axis=0, tiled=True)]
    all_to_all x2 -> x1, waiting for transfers between devices: 19.2 us -> 0.01 us  [body(): lax.all_to_all(sent.reshape(fsdp, Q, columns), FSDP, split_axis=0, concat...]
    unnamed x38 -> x39, local copies, waits for them, and re-layouts: 9.72 us -> 18.6 us
    all_to_all x2 -> x1, starting transfers between devices: 25.6 us -> 17.3 us  [body(): lax.all_to_all(sent.reshape(fsdp, Q, columns), FSDP, split_axis=0, concat...]
    pallas_call x2 -> x4, Pallas kernels: 9.59 us -> 17.3 us  [the longest x1 10.2 us: body(): pl.pallas_call(functools.partial(base_kernel, size_x, size_z), out_shape=...]
  transfers between devices with their start and end apart: 10 -> 20, of which waited for: 4 -> 4; matrix products, arithmetic and copies ran while one was open for 0% -> 2% of each run, Pallas kernels for 8% -> 8%
where the time goes in v3:
time: 269 us; the launch traced here: 267 us
  starting transfers between devices  125 us (46%)
  waiting for transfers between devices  71.6 us (27%)
  Pallas kernels  27.7 us (10%)
  blocking collectives  22.8 us (8%)
  local copies, waits for them, and re-layouts  19.2 us (7%)
    ppermute x7, waiting for transfers between devices, body(): parts.append(lax.ppermute(column, 'z', climb))  71.6 us
    ppermute x4, starting transfers between devices, body(): other.append(lax.ppermute(own[k], 'core', SWAP))  48.7 us
    all_gather x1, blocking collectives, body(): column = lax.all_gather(frozen_value_weight, COLUMN, axis=0, tiled=True)  22.8 us
    ppermute x7, starting transfers between devices, body(): parts.append(lax.ppermute(column, 'z', climb))  21.2 us
    unnamed x39, local copies, waits for them, and re-layouts  18.6 us
    all_to_all x1, starting transfers between devices, body(): lax.all_to_all(back.reshape(fsdp, Q, half), FSDP, split_axis=0, concat_ax...  18.3 us
    all_to_all x1, starting transfers between devices, body(): lax.all_to_all(sent.reshape(fsdp, Q, columns), FSDP, split_axis=0, concat...  17.3 us
    pallas_call x1, Pallas kernels, body(): pl.pallas_call(functools.partial(base_kernel, size_x, size_z), out_shape=...  10.2 us
  transfers between devices with their start and end apart: 20, of which 4 were waited for; matrix products, arithmetic and copies ran while one was open for 2% of the time, Pallas kernels for 8%

profile of v3, /device:TPU:1, one launch (start us, length us, event | category | flops | bytes accessed | tf_op | source)
XLA Modules:
  0.0 267.4 jit_solution(674087936678272211)
XLA Ops:
  0.6 22.8 %all_gather.3 = bf16[128,512]{1,0:T(8,128)(2,1)} all-gather(bf16[16,512]{1,0:T(8,128)(2,1)} %param.11), channel_id=1, replica_groups=mesh['x'=4,'z'=8,'yh'=2,'yl'=4,'core'=2] {'yh','yl'}, dimensions={0}, use_global_device_ids=true | all-gather | bytes 147456 | tf_op jit(solution)/shard_map/all_gather | solution.py:256
  23.5 1.6 copy-done
  25.1 0.9 copy-done.11
  27.3 5.8 %dispatch.1 = (bf16[512,3328]{1,0:T(8,128)(2,1)S(1)}, bf16[2,512,128]{2,1,0:T(8,128)(2,1)S(1)}) custom-call(s32[64]{0:T(128)S(1)} %copy-done.13, s32[1,128]{1,0:T(1,128)S(1)} %bitcast.25, bf16[128,8192]{1,0:T(8,128)(2,1)S(1)} %copy-done, bf16[128,512]{1,0:T(8,128)(2,1)S(1)} %copy-done.11), custom_call_target="tpu_custom_call" | custom-call | tf_op jit(solution)/shard_map/dispatch/pallas_call | solution.py:257
  33.1 1.7 copy-done.1
  34.8 0.7 copy-done.8
  35.5 17.3 %all-to-all-start = ((bf16[64,8,3328]{2,1,0:T(8,128)(2,1)}), bf16[64,8,3328]{2,1,0:T(8,128)(2,1)S(1)}, u32[]{:S(2)}, u32[]{:S(2)}) async-start(bf16[64,8,3328]{2,1,0:T(8,128)(2,1)} %bitcast.20), calls=%async_computation | async-start | bytes 6815744 | tf_op jit(solution)/shard_map/all_to_all | solution.py:289
  52.8 2.9 %collective-permute-start = (bf16[128,512]{1,0:T(8,128)(2,1)}, bf16[128,512]{1,0:T(8,128)(2,1)S(1)}, u32[]{:S(2)}, u32[]{:S(2)}) collective-permute-start(bf16[128,512]{1,0:T(8,128)(2,1)} %all_gather.3), channel_id=1, source_target_pairs={{0,16},{16,32},{32,48},{48,64},{64,80},{80,96},{96,112},{112,0},{1... | collective-permute-start | bytes 393224 | tf_op jit(solution)/shard_map/ppermute | solution.py:273
  55.7 3.6 %collective-permute-start.6 = (bf16[128,512]{1,0:T(8,128)(2,1)}, bf16[128,512]{1,0:T(8,128)(2,1)S(1)}, u32[]{:S(2)}, u32[]{:S(2)}) collective-permute-start(bf16[128,512]{1,0:T(8,128)(2,1)} %all_gather.3), channel_id=1, source_target_pairs={{0,112},{16,0},{32,16},{48,32},{64,48},{80,64},{96,80},{112,96},{1... | collective-permute-start | bytes 393224 | tf_op jit(solution)/shard_map/ppermute | solution.py:273
  59.3 3.8 %collective-permute-start.5 = (bf16[128,512]{1,0:T(8,128)(2,1)}, bf16[128,512]{1,0:T(8,128)(2,1)S(1)}, u32[]{:S(2)}, u32[]{:S(2)}) collective-permute-start(bf16[128,512]{1,0:T(8,128)(2,1)} %all_gather.3), channel_id=1, source_target_pairs={{0,96},{16,112},{32,0},{48,16},{64,32},{80,48},{96,64},{112,80},{1... | collective-permute-start | bytes 393224 | tf_op jit(solution)/shard_map/ppermute | solution.py:273
  63.1 4.9 %collective-permute-start.4 = (bf16[128,512]{1,0:T(8,128)(2,1)}, bf16[128,512]{1,0:T(8,128)(2,1)S(1)}, u32[]{:S(2)}, u32[]{:S(2)}) collective-permute-start(bf16[128,512]{1,0:T(8,128)(2,1)} %all_gather.3), channel_id=1, source_target_pairs={{0,80},{16,96},{32,112},{48,0},{64,16},{80,32},{96,48},{112,64},{1... | collective-permute-start | bytes 393224 | tf_op jit(solution)/shard_map/ppermute | solution.py:273
  68.1 2.2 collective-permute-start.1
  70.2 1.6 constant_dynamic-update-slice_fusion.7
  71.8 38.5 %collective-permute-done = bf16[128,512]{1,0:T(8,128)(2,1)S(1)} collective-permute-done((bf16[128,512]{1,0:T(8,128)(2,1)}, bf16[128,512]{1,0:T(8,128)(2,1)S(1)}, u32[]{:S(2)}, u32[]{:S(2)}) %collective-permute-start) | collective-permute-done | bytes 131104 | tf_op jit(solution)/shard_map/ppermute | solution.py:273
  110.3 1.9 collective-permute-start.2
  112.8 26.4 %collective-permute-done.1 = bf16[128,512]{1,0:T(8,128)(2,1)S(1)} collective-permute-done((bf16[128,512]{1,0:T(8,128)(2,1)}, bf16[128,512]{1,0:T(8,128)(2,1)S(1)}, u32[]{:S(2)}, u32[]{:S(2)}) %collective-permute-start.1) | collective-permute-done | bytes 131104 | tf_op jit(solution)/shard_map/ppermute | solution.py:273
  139.2 1.9 collective-permute-start.3
  141.8 1.1 collective-permute-done.2
  143.0 0.7 constant_dynamic-update-slice_fusion.4
  143.6 5.5 %collective-permute-done.3 = bf16[128,512]{1,0:T(8,128)(2,1)S(1)} collective-permute-done((bf16[128,512]{1,0:T(8,128)(2,1)}, bf16[128,512]{1,0:T(8,128)(2,1)S(1)}, u32[]{:S(2)}, u32[]{:S(2)}) %collective-permute-start.3) | collective-permute-done | bytes 131104 | tf_op jit(solution)/shard_map/ppermute | solution.py:273
  149.2 0.7 constant_dynamic-update-slice_fusion.3
  150.5 0.7 constant_dynamic-update-slice_fusion.1
  151.2 0.7 constant_dynamic-update-slice_fusion
  151.8 3.7 %collective-permute-start.10 = (bf16[64,16,512]{2,1,0:T(8,128)(2,1)}, bf16[64,16,512]{2,1,0:T(8,128)(2,1)}, u32[]{:S(2)}, u32[]{:S(2)}) collective-permute-start(bf16[64,16,512]{2,1,0:T(8,128)(2,1)} %bitcast.5.refs_0_), channel_id=1, source_target_pairs={{0,384},{128,0},{256,128},{384,256},{1,385},{129,1},{257,129},{385... | collective-permute-start | bytes 3145736 | tf_op jit(solution)/shard_map/ppermute | solution.py:278
  155.5 2.4 collective-permute-start.9
  157.9 2.5 collective-permute-start.8
  160.4 15.4 %collective-permute-start.7 = (bf16[64,16,512]{2,1,0:T(8,128)(2,1)}, bf16[64,16,512]{2,1,0:T(8,128)(2,1)}, u32[]{:S(2)}, u32[]{:S(2)}) collective-permute-start(bf16[64,16,512]{2,1,0:T(8,128)(2,1)} %bitcast.5.refs_0_), channel_id=1, source_target_pairs={{0,1},{1,0},{2,3},{3,2},{4,5},{5,4},{6,7},{7,6},{8,9},{9,8},{10,11... | collective-permute-start | bytes 3145736 | tf_op jit(solution)/shard_map/ppermute | solution.py:281
  175.8 27.7 %collective-permute-start.13 = (bf16[64,16,512]{2,1,0:T(8,128)(2,1)}, bf16[64,16,512]{2,1,0:T(8,128)(2,1)}, u32[]{:S(2)}, u32[]{:S(2)}) collective-permute-start(bf16[64,16,512]{2,1,0:T(8,128)(2,1)} %collective-permute-done.10.refs_3_), channel_id=1, source_target_pairs={{0,1},{1,0},{2,3},{3,2},{4,5},{5,4},{6,7},{7,6},{8,9},{9,8},{10,11... | collective-permute-start | bytes 3145736 | tf_op jit(solution)/shard_map/ppermute | solution.py:281
  203.6 1.9 collective-permute-start.12
  205.5 3.6 %collective-permute-start.11 = (bf16[64,16,512]{2,1,0:T(8,128)(2,1)}, bf16[64,16,512]{2,1,0:T(8,128)(2,1)}, u32[]{:S(2)}, u32[]{:S(2)}) collective-permute-start(bf16[64,16,512]{2,1,0:T(8,128)(2,1)} %collective-permute-done.8.refs_1_), channel_id=1, source_target_pairs={{0,1},{1,0},{2,3},{3,2},{4,5},{5,4},{6,7},{7,6},{8,9},{9,8},{10,11... | collective-permute-start | bytes 3145736 | tf_op jit(solution)/shard_map/ppermute | solution.py:281
  209.3 1.2 copy-done.4
  210.5 2.2 correct.1
  212.7 0.7 copy-done.10
  213.4 3.8 %grads.1 = (f32[256,1152]{1,0:T(8,128)S(1)}, bf16[256,1152]{1,0:T(8,128)(2,1)}) custom-call(s32[4]{0:T(128)S(1)} %pad_add_fusion.where_ref, bf16[512,3328]{1,0:T(8,128)(2,1)S(1)} %bitcast.19, bf16[64,512]{1,0:T(8,128)(2,1)S(1)} %bitcast.23, bf16[512,128]{1,0:T(8,128)(2,1)S(1)} %get-tuple-element.22.low_ref), custom_call_target="tpu_custom_call" | custom-call | tf_op jit(solution)/shard_map/grads/pallas_call | solution.py:309
  217.2 1.0 copy-done.2
  218.3 1.9 collective-permute-start.14
  220.2 18.3 %all-to-all-start.1 = ((bf16[64,8,256]{2,1,0:T(8,128)(2,1)}), bf16[64,8,256]{2,1,0:T(8,128)(2,1)}, u32[]{:S(2)}, u32[]{:S(2)}) async-start(bf16[64,8,256]{2,1,0:T(8,128)(2,1)} %bitcast.24), calls=%async_computation.1 | async-start | bytes 524288 | tf_op jit(solution)/shard_map/all_to_all | solution.py:305
  238.5 1.3 copy-done.3
  239.8 1.4 middle.1
  241.2 1.9 collective-permute-start.15
  243.1 4.1 %collective-permute-start.16 = (bf16[64,1152]{1,0:T(8,128)(2,1)}, bf16[64,1152]{1,0:T(8,128)(2,1)}, u32[]{:S(2)}, u32[]{:S(2)}) collective-permute-start(bf16[64,1152]{1,0:T(8,128)(2,1)} %get-tuple-element.27), channel_id=1, source_target_pairs={{0,4},{2,6},{4,0},{6,2},{1,5},{3,7},{5,1},{7,3},{8,12},{10,14},{12... | collective-permute-start | bytes 442376 | tf_op jit(solution)/shard_map/ppermute | solution.py:334
  247.2 3.0 %collective-permute-start.17 = (bf16[64,1152]{1,0:T(8,128)(2,1)}, bf16[64,1152]{1,0:T(8,128)(2,1)}, u32[]{:S(2)}, u32[]{:S(2)}) collective-permute-start(bf16[64,1152]{1,0:T(8,128)(2,1)} %get-tuple-element.28), channel_id=1, source_target_pairs={{0,6},{2,0},{4,2},{6,4},{1,7},{3,1},{5,3},{7,5},{8,14},{10,8},{12,... | collective-permute-start | bytes 442376 | tf_op jit(solution)/shard_map/ppermute | solution.py:334
  250.8 0.7 copy-done.12
  251.5 10.2 %base.1.base_ref = f32[128,512]{1,0:T(8,128)S(1)} custom-call(s32[4]{0:T(128)S(1)} %pad_add_fusion.where_ref, bf16[128,8192]{1,0:T(8,128)(2,1)} %tokens_ref.3, bf16[1,512]{1,0:T(2,128)(2,1)S(1)} %reshape.27.bias_ref, f32[8,128]{1,0:T(8,128)S(1)} %copy-done.12, bf16[64,16,512]{2,1,0:T(8,128)(2,1)} %bitcast.5.refs_0_, ...), custom_call_target="tpu_custom_call" | custom-call | tf_op jit(solution)/shard_map/base/pallas_call | solution.py:335
  261.8 0.9 copy-done.9
  262.7 1.9 place.1
  264.6 1.0 copy-done.6
  265.6 1.8 finish.1
  (43 shorter events, 4.0 us)
Async XLA Ops:
  23.5 1.6 copy-start
  25.1 0.9 copy-start.11
  26.0 0.7 copy-start.13
  26.6 0.7 copy-start.14
  33.1 1.7 copy-start.1
  34.8 0.7 copy-start.8
  35.5 173.8 %copy-start.7 = (bf16[1,64,512]{2,1,0:T(8,128)(2,1)S(1)}, bf16[1,64,512]{2,1,0:T(8,128)(2,1)}, u32[]{:S(2)}) copy-start(bf16[1,64,512]{2,1,0:T(8,128)(2,1)} %param.14) | copy-start | bytes 196612
  35.5 173.8 %all-to-all-start = ((bf16[64,8,3328]{2,1,0:T(8,128)(2,1)}), bf16[64,8,3328]{2,1,0:T(8,128)(2,1)S(1)}, u32[]{:S(2)}, u32[]{:S(2)}) async-start(bf16[64,8,3328]{2,1,0:T(8,128)(2,1)} %bitcast.20), calls=%async_computation | async-start | bytes 6815744 | tf_op jit(solution)/shard_map/all_to_all | solution.py:289
  52.8 57.5 %collective-permute-start = (bf16[128,512]{1,0:T(8,128)(2,1)}, bf16[128,512]{1,0:T(8,128)(2,1)S(1)}, u32[]{:S(2)}, u32[]{:S(2)}) collective-permute-start(bf16[128,512]{1,0:T(8,128)(2,1)} %all_gather.3), channel_id=1, source_target_pairs={{0,16},{16,32},{32,48},{48,64},{64,80},{80,96},{96,112},{112,0},{1... | collective-permute-start | bytes 393224 | tf_op jit(solution)/shard_map/ppermute | solution.py:273
  55.7 95.5 %collective-permute-start.6 = (bf16[128,512]{1,0:T(8,128)(2,1)}, bf16[128,512]{1,0:T(8,128)(2,1)S(1)}, u32[]{:S(2)}, u32[]{:S(2)}) collective-permute-start(bf16[128,512]{1,0:T(8,128)(2,1)} %all_gather.3), channel_id=1, source_target_pairs={{0,112},{16,0},{32,16},{48,32},{64,48},{80,64},{96,80},{112,96},{1... | collective-permute-start | bytes 393224 | tf_op jit(solution)/shard_map/ppermute | solution.py:273
  59.3 91.2 %collective-permute-start.5 = (bf16[128,512]{1,0:T(8,128)(2,1)}, bf16[128,512]{1,0:T(8,128)(2,1)S(1)}, u32[]{:S(2)}, u32[]{:S(2)}) collective-permute-start(bf16[128,512]{1,0:T(8,128)(2,1)} %all_gather.3), channel_id=1, source_target_pairs={{0,96},{16,112},{32,0},{48,16},{64,32},{80,48},{96,64},{112,80},{1... | collective-permute-start | bytes 393224 | tf_op jit(solution)/shard_map/ppermute | solution.py:273
  63.1 86.7 %collective-permute-start.4 = (bf16[128,512]{1,0:T(8,128)(2,1)}, bf16[128,512]{1,0:T(8,128)(2,1)S(1)}, u32[]{:S(2)}, u32[]{:S(2)}) collective-permute-start(bf16[128,512]{1,0:T(8,128)(2,1)} %all_gather.3), channel_id=1, source_target_pairs={{0,80},{16,96},{32,112},{48,0},{64,16},{80,32},{96,48},{112,64},{1... | collective-permute-start | bytes 393224 | tf_op jit(solution)/shard_map/ppermute | solution.py:273
  68.1 71.2 %collective-permute-start.1 = (bf16[128,512]{1,0:T(8,128)(2,1)}, bf16[128,512]{1,0:T(8,128)(2,1)S(1)}, u32[]{:S(2)}, u32[]{:S(2)}) collective-permute-start(bf16[128,512]{1,0:T(8,128)(2,1)} %all_gather.3), channel_id=1, source_target_pairs={{0,32},{16,48},{32,64},{48,80},{64,96},{80,112},{96,0},{112,16},{1... | collective-permute-start | bytes 393224 | tf_op jit(solution)/shard_map/ppermute | solution.py:273
  110.3 32.7 %collective-permute-start.2 = (bf16[128,512]{1,0:T(8,128)(2,1)}, bf16[128,512]{1,0:T(8,128)(2,1)S(1)}, u32[]{:S(2)}, u32[]{:S(2)}) collective-permute-start(bf16[128,512]{1,0:T(8,128)(2,1)} %all_gather.3), channel_id=1, source_target_pairs={{0,48},{16,64},{32,80},{48,96},{64,112},{80,0},{96,16},{112,32},{1... | collective-permute-start | bytes 393224 | tf_op jit(solution)/shard_map/ppermute | solution.py:273
  139.2 9.9 %collective-permute-start.3 = (bf16[128,512]{1,0:T(8,128)(2,1)}, bf16[128,512]{1,0:T(8,128)(2,1)S(1)}, u32[]{:S(2)}, u32[]{:S(2)}) collective-permute-start(bf16[128,512]{1,0:T(8,128)(2,1)} %all_gather.3), channel_id=1, source_target_pairs={{0,64},{16,80},{32,96},{48,112},{64,0},{80,16},{96,32},{112,48},{1... | collective-permute-start | bytes 393224 | tf_op jit(solution)/shard_map/ppermute | solution.py:273
  151.8 24.0 %collective-permute-start.10 = (bf16[64,16,512]{2,1,0:T(8,128)(2,1)}, bf16[64,16,512]{2,1,0:T(8,128)(2,1)}, u32[]{:S(2)}, u32[]{:S(2)}) collective-permute-start(bf16[64,16,512]{2,1,0:T(8,128)(2,1)} %bitcast.5.refs_0_), channel_id=1, source_target_pairs={{0,384},{128,0},{256,128},{384,256},{1,385},{129,1},{257,129},{385... | collective-permute-start | bytes 3145736 | tf_op jit(solution)/shard_map/ppermute | solution.py:278
  155.5 48.1 %collective-permute-start.9 = (bf16[64,16,512]{2,1,0:T(8,128)(2,1)}, bf16[64,16,512]{2,1,0:T(8,128)(2,1)}, u32[]{:S(2)}, u32[]{:S(2)}) collective-permute-start(bf16[64,16,512]{2,1,0:T(8,128)(2,1)} %bitcast.5.refs_0_), channel_id=1, source_target_pairs={{0,256},{128,384},{256,0},{384,128},{1,257},{129,385},{257,1},{385... | collective-permute-start | bytes 3145736 | tf_op jit(solution)/shard_map/ppermute | solution.py:278
  157.9 47.6 %collective-permute-start.8 = (bf16[64,16,512]{2,1,0:T(8,128)(2,1)}, bf16[64,16,512]{2,1,0:T(8,128)(2,1)}, u32[]{:S(2)}, u32[]{:S(2)}) collective-permute-start(bf16[64,16,512]{2,1,0:T(8,128)(2,1)} %bitcast.5.refs_0_), channel_id=1, source_target_pairs={{0,128},{128,256},{256,384},{384,0},{1,129},{129,257},{257,385},{3... | collective-permute-start | bytes 3145736 | tf_op jit(solution)/shard_map/ppermute | solution.py:278
  160.4 82.6 %collective-permute-start.7 = (bf16[64,16,512]{2,1,0:T(8,128)(2,1)}, bf16[64,16,512]{2,1,0:T(8,128)(2,1)}, u32[]{:S(2)}, u32[]{:S(2)}) collective-permute-start(bf16[64,16,512]{2,1,0:T(8,128)(2,1)} %bitcast.5.refs_0_), channel_id=1, source_target_pairs={{0,1},{1,0},{2,3},{3,2},{4,5},{5,4},{6,7},{7,6},{8,9},{9,8},{10,11... | collective-permute-start | bytes 3145736 | tf_op jit(solution)/shard_map/ppermute | solution.py:281
  175.8 71.4 %collective-permute-start.13 = (bf16[64,16,512]{2,1,0:T(8,128)(2,1)}, bf16[64,16,512]{2,1,0:T(8,128)(2,1)}, u32[]{:S(2)}, u32[]{:S(2)}) collective-permute-start(bf16[64,16,512]{2,1,0:T(8,128)(2,1)} %collective-permute-done.10.refs_3_), channel_id=1, source_target_pairs={{0,1},{1,0},{2,3},{3,2},{4,5},{5,4},{6,7},{7,6},{8,9},{9,8},{10,11... | collective-permute-start | bytes 3145736 | tf_op jit(solution)/shard_map/ppermute | solution.py:281
  203.6 47.2 %collective-permute-start.12 = (bf16[64,16,512]{2,1,0:T(8,128)(2,1)}, bf16[64,16,512]{2,1,0:T(8,128)(2,1)}, u32[]{:S(2)}, u32[]{:S(2)}) collective-permute-start(bf16[64,16,512]{2,1,0:T(8,128)(2,1)} %collective-permute-done.9.refs_2_), channel_id=1, source_target_pairs={{0,1},{1,0},{2,3},{3,2},{4,5},{5,4},{6,7},{7,6},{8,9},{9,8},{10,11... | collective-permute-start | bytes 3145736 | tf_op jit(solution)/shard_map/ppermute | solution.py:281
  205.5 45.3 %collective-permute-start.11 = (bf16[64,16,512]{2,1,0:T(8,128)(2,1)}, bf16[64,16,512]{2,1,0:T(8,128)(2,1)}, u32[]{:S(2)}, u32[]{:S(2)}) collective-permute-start(bf16[64,16,512]{2,1,0:T(8,128)(2,1)} %collective-permute-done.8.refs_1_), channel_id=1, source_target_pairs={{0,1},{1,0},{2,3},{3,2},{4,5},{5,4},{6,7},{7,6},{8,9},{9,8},{10,11... | collective-permute-start | bytes 3145736 | tf_op jit(solution)/shard_map/ppermute | solution.py:281
  209.3 1.2 copy-start.4
  212.7 0.7 copy-start.10
  213.4 36.8 %copy-start.15 = (bf16[512]{0:T(512)(128)(2,1)S(1)}, bf16[512]{0:T(512)(128)(2,1)}, u32[]{:S(2)}) copy-start(bf16[512]{0:T(512)(128)(2,1)} %param.12) | copy-start | bytes 3076
  217.2 1.0 copy-start.2
  218.3 20.2 %collective-permute-start.14 = (bf16[256,1152]{1,0:T(8,128)(2,1)}, bf16[256,1152]{1,0:T(8,128)(2,1)S(1)}, u32[]{:S(2)}, u32[]{:S(2)}) collective-permute-start(bf16[256,1152]{1,0:T(8,128)(2,1)} %get-tuple-element.24), channel_id=1, source_target_pairs={{0,1},{1,0},{2,3},{3,2},{4,5},{5,4},{6,7},{7,6},{8,9},{9,8},{10,11... | collective-permute-start | bytes 1769480 | tf_op jit(solution)/shard_map/ppermute | solution.py:321
  220.2 41.5 %all-to-all-start.1 = ((bf16[64,8,256]{2,1,0:T(8,128)(2,1)}), bf16[64,8,256]{2,1,0:T(8,128)(2,1)}, u32[]{:S(2)}, u32[]{:S(2)}) async-start(bf16[64,8,256]{2,1,0:T(8,128)(2,1)} %bitcast.24), calls=%async_computation.1 | async-start | bytes 524288 | tf_op jit(solution)/shard_map/all_to_all | solution.py:305
  238.5 1.3 copy-start.3
  241.2 9.7 %copy-start.5 = (f32[64,1152]{1,0:T(8,128)}, f32[64,1152]{1,0:T(8,128)S(1)}, u32[]{:S(2)}) copy-start(f32[64,1152]{1,0:T(8,128)S(1)} %get-tuple-element.25.mine_ref) | copy-start | bytes 884740
  241.2 23.4 %collective-permute-start.15 = (bf16[64,1152]{1,0:T(8,128)(2,1)}, bf16[64,1152]{1,0:T(8,128)(2,1)}, u32[]{:S(2)}, u32[]{:S(2)}) collective-permute-start(bf16[64,1152]{1,0:T(8,128)(2,1)} %get-tuple-element.26), channel_id=1, source_target_pairs={{0,2},{2,4},{4,6},{6,0},{1,3},{3,5},{5,7},{7,1},{8,10},{10,12},{12... | collective-permute-start | bytes 442376 | tf_op jit(solution)/shard_map/ppermute | solution.py:334
  243.1 21.5 %collective-permute-start.16 = (bf16[64,1152]{1,0:T(8,128)(2,1)}, bf16[64,1152]{1,0:T(8,128)(2,1)}, u32[]{:S(2)}, u32[]{:S(2)}) collective-permute-start(bf16[64,1152]{1,0:T(8,128)(2,1)} %get-tuple-element.27), channel_id=1, source_target_pairs={{0,4},{2,6},{4,0},{6,2},{1,5},{3,7},{5,1},{7,3},{8,12},{10,14},{12... | collective-permute-start | bytes 442376 | tf_op jit(solution)/shard_map/ppermute | solution.py:334
  247.2 17.4 %collective-permute-start.17 = (bf16[64,1152]{1,0:T(8,128)(2,1)}, bf16[64,1152]{1,0:T(8,128)(2,1)}, u32[]{:S(2)}, u32[]{:S(2)}) collective-permute-start(bf16[64,1152]{1,0:T(8,128)(2,1)} %get-tuple-element.28), channel_id=1, source_target_pairs={{0,6},{2,0},{4,2},{6,4},{1,7},{3,1},{5,3},{7,5},{8,14},{10,8},{12,... | collective-permute-start | bytes 442376 | tf_op jit(solution)/shard_map/ppermute | solution.py:334
  250.8 0.7 copy-start.12
  261.8 1.0 copy-start.9
  264.6 1.0 copy-start.6

commit v4 on v3

--- a/solution.py
+++ b/solution.py
@@ -13,7 +13,7 @@
 Q = 8
 FSDP = ("x", "z", "yh")
 DP = ("yl", "core")
-COLUMN = ("yh", "yl")
+PLANE = ("z", "yh", "yl")
 SWAP = ((0, 1), (1, 0))
 F32 = jnp.float32
 BF16 = jnp.bfloat16
@@ -184,7 +184,7 @@
     )[:, :rank]
 
 
-def base_kernel(size_x, size_z, where_ref, tokens_ref, bias_ref, gate_ref, *refs):
+def base_kernel(size_x, size_z, where_ref, tokens_ref, bias_ref, *refs):
     own, other, base_ref = refs[:size_x], refs[size_x : 2 * size_x], refs[-1]
     groups, block, out_width = own[0].shape
     step = groups // size_z
@@ -196,7 +196,6 @@
 
         @pl.loop(0, size_z)
         def _(i):
-            from_z = lax.rem(where_ref[1] + size_z - i, size_z)
             mine = own[k][pl.ds(i * step, step)]
             theirs = other[k][pl.ds(i * step, step)]
             low = jnp.where(first, mine, theirs)
@@ -205,12 +204,8 @@
                 [low.reshape(step, 1, block, out_width), high.reshape(step, 1, block, out_width)],
                 axis=1,
             ).reshape(rows, out_width)
-            columns = pl.ds(pl.multiple_of((from_x * size_z + from_z) * rows, rows), rows)
+            columns = pl.ds(pl.multiple_of((from_x * size_z + i) * rows, rows), rows)
             base_ref[...] += nn(tokens_ref[:, columns], weight)
-
-
-def gate_kernel(*refs):
-    refs[-1][...] = jnp.zeros_like(refs[-1])
 
 
 def place_kernel(base_ref, place_ref, back_ref, values_ref):
@@ -253,7 +248,14 @@
     rows = fsdp * Q
     columns = SLOTS * chunk + half
 
-    column = lax.all_gather(frozen_value_weight, COLUMN, axis=0, tiled=True)
+    plane = lax.axis_size(PLANE)
+    piece = lax.all_to_all(
+        jnp.broadcast_to(frozen_value_weight[None], (plane, *frozen_value_weight.shape)),
+        PLANE,
+        split_axis=0,
+        concat_axis=0,
+        tiled=True,
+    )
     sent, place = pl.pallas_call(
         dispatch_kernel,
         out_shape=(
@@ -266,12 +268,7 @@
         compiler_params=PARAMS,
         name="dispatch",
     )(adapter_storage_index, token_adapter_index.reshape(1, count), tokens, cotangent)
-    sent, column = lax.optimization_barrier((sent, column))
-    parts = [column]
-    for k in range(1, size_z):
-        climb = [(i, (i + k) % size_z) for i in range(size_z)]
-        parts.append(lax.ppermute(column, "z", climb))
-    piece = jnp.concatenate(parts, axis=0).reshape(-1, *frozen_value_weight.shape)
+    sent, piece = lax.optimization_barrier((sent, piece))
     own = [piece]
     for k in range(1, size_x):
         shift = [(i, (i + k) % size_x) for i in range(size_x)]
@@ -279,13 +276,6 @@
     other = []
     for k in range(size_x):
         other.append(lax.ppermute(own[k], "core", SWAP))
-    gate = pl.pallas_call(
-        gate_kernel,
-        out_shape=jax.ShapeDtypeStruct((8, 128), F32),
-        in_specs=[pl.BlockSpec(memory_space=pl.ANY)],
-        out_specs=vmem(1)[0],
-        name="gate",
-    )(other[0])
     arrived = lax.all_to_all(
         sent.reshape(fsdp, Q, columns), FSDP, split_axis=0, concat_axis=0, tiled=True
     ).reshape(rows, columns)
@@ -335,11 +325,11 @@
     base = pl.pallas_call(
         functools.partial(base_kernel, size_x, size_z),
         out_shape=jax.ShapeDtypeStruct((count, out_width), F32),
-        in_specs=smem + vmem(3 + 2 * size_x),
+        in_specs=smem + vmem(2 + 2 * size_x),
         out_specs=vmem(1)[0],
         compiler_params=PARAMS,
         name="base",
-    )(where, tokens, frozen_value_bias.reshape(1, out_width), gate, *own, *other)
+    )(where, tokens, frozen_value_bias.reshape(1, out_width), *own, *other)
     values = pl.pallas_call(
         place_kernel,
         out_shape=jax.ShapeDtypeStruct((count, out_width), BF16),

time: 269 us -> 202 us (0.75)
  starting transfers between devices: 125 us -> 79.6 us
  blocking collectives: 22.8 us -> 0 us
  waiting for transfers between devices: 71.6 us -> 81.9 us
  local copies, waits for them, and re-layouts: 19.2 us -> 13 us
  Pallas kernels: 27.7 us -> 24.8 us
    ppermute x7 -> x0, waiting for transfers between devices: 71.6 us -> none  [body(): parts.append(lax.ppermute(column, 'z', climb))]
    ppermute x3, waiting for transfers between devices: 0.01 us -> 64.8 us  [body(): own.append(lax.ppermute(piece, 'x', shift))]
    ppermute x4, starting transfers between devices: 48.7 us -> 16.4 us  [body(): other.append(lax.ppermute(own[k], 'core', SWAP))]
    all_gather x1 -> x0, blocking collectives: 22.8 us -> none  [body(): column = lax.all_gather(frozen_value_weight, COLUMN, axis=0, tiled=True)]
    ppermute x7 -> x0, starting transfers between devices: 21.2 us -> none  [body(): parts.append(lax.ppermute(column, 'z', climb))]
    all_to_all x0 -> x1, starting transfers between devices: none -> 17.1 us  [body(): lax.all_to_all(jnp.broadcast_to(frozen_value_weight[None], (plane, *froze...]
    all_to_all x0 -> x1, waiting for transfers between devices: none -> 17.1 us  [body(): lax.all_to_all(jnp.broadcast_to(frozen_value_weight[None], (plane, *froze...]
    unnamed x39 -> x30, local copies, waits for them, and re-layouts: 18.6 us -> 11 us
  transfers between devices with their start and end apart: 20 -> 14, of which waited for: 4 -> 3; matrix products, arithmetic and copies ran while one was open for 2% -> 0% of each run, Pallas kernels for 8% -> 12%
where the time goes in v4:
time: 202 us; the launch traced here: 200 us
  waiting for transfers between devices  81.9 us (41%)
  starting transfers between devices  79.6 us (39%)
  Pallas kernels  24.8 us (12%)
  local copies, waits for them, and re-layouts  13 us (6%)
    ppermute x3, waiting for transfers between devices, body(): own.append(lax.ppermute(piece, 'x', shift))  64.8 us
    all_to_all x1, starting transfers between devices, body(): lax.all_to_all(jnp.broadcast_to(frozen_value_weight[None], (plane, *froze...  17.1 us
    all_to_all x1, waiting for transfers between devices, body(): lax.all_to_all(jnp.broadcast_to(frozen_value_weight[None], (plane, *froze...  17.1 us
    ppermute x4, starting transfers between devices, body(): other.append(lax.ppermute(own[k], 'core', SWAP))  16.4 us
    all_to_all x1, starting transfers between devices, body(): lax.all_to_all(back.reshape(fsdp, Q, half), FSDP, split_axis=0, concat_ax...  14 us
    unnamed x30, local copies, waits for them, and re-layouts  11 us
    ppermute x3, starting transfers between devices, body(): arrivals.append(lax.ppermute(sums[k - 1], 'yl', rise))  10.9 us
    all_to_all x1, starting transfers between devices, body(): lax.all_to_all(sent.reshape(fsdp, Q, columns), FSDP, split_axis=0, concat...  10 us
  transfers between devices with their start and end apart: 14, of which 3 were waited for; matrix products, arithmetic and copies ran while one was open for 0% of the time, Pallas kernels for 12%

profile of v4, /device:TPU:1, one launch (start us, length us, event | category | flops | bytes accessed | tf_op | source)
XLA Modules:
  0.0 200.3 jit_solution(1266057248727624203)
XLA Ops:
  0.6 0.0 copy-start
  0.6 2.0 broadcast_in_dim.12
  2.6 17.1 %all-to-all-start = ((bf16[64,16,512]{2,1,0:T(8,128)(2,1)}), bf16[64,16,512]{2,1,0:T(8,128)(2,1)S(1)}, u32[]{:S(2)}, u32[]{:S(2)}) async-start(bf16[64,16,512]{2,1,0:T(8,128)(2,1)} %broadcast_in_dim.12), calls=%async_computation | async-start | bytes 2097152 | tf_op jit(solution)/shard_map/all_to_all | solution.py:252
  19.7 0.0 copy-start.11
  19.8 0.9 copy-done.11
  20.7 0.7 copy-done.12
  21.3 0.7 copy-done.13
  22.0 5.8 %dispatch.1 = (bf16[512,3328]{1,0:T(8,128)(2,1)S(1)}, bf16[2,512,128]{2,1,0:T(8,128)(2,1)S(1)}) custom-call(s32[64]{0:T(128)S(1)} %copy-done.12, s32[1,128]{1,0:T(1,128)S(1)} %bitcast.25, bf16[128,8192]{1,0:T(8,128)(2,1)S(1)} %copy-done, bf16[128,512]{1,0:T(8,128)(2,1)S(1)} %copy-done.11), custom_call_target="tpu_custom_call" | custom-call | tf_op jit(solution)/shard_map/dispatch/pallas_call | solution.py:259
  27.8 1.7 copy-done.3
  29.4 0.7 copy-done.8
  30.1 17.1 %all-to-all-done.refs_0_ = bf16[64,16,512]{2,1,0:T(8,128)(2,1)S(1)} async-done(((bf16[64,16,512]{2,1,0:T(8,128)(2,1)}), bf16[64,16,512]{2,1,0:T(8,128)(2,1)S(1)}, u32[]{:S(2)}, u32[]{:S(2)}) %all-to-all-start) | async-done | bytes 1048608 | tf_op jit(solution)/shard_map/all_to_all | solution.py:252
  47.2 1.0 copy-done.1
  48.2 10.0 %all-to-all-start.1 = ((bf16[64,8,3328]{2,1,0:T(8,128)(2,1)}), bf16[64,8,3328]{2,1,0:T(8,128)(2,1)S(1)}, u32[]{:S(2)}, u32[]{:S(2)}) async-start(bf16[64,8,3328]{2,1,0:T(8,128)(2,1)} %bitcast.19), calls=%async_computation.1 | async-start | bytes 6815744 | tf_op jit(solution)/shard_map/all_to_all | solution.py:279
  58.2 4.3 %collective-permute-start.2 = (bf16[64,16,512]{2,1,0:T(8,128)(2,1)}, bf16[64,16,512]{2,1,0:T(8,128)(2,1)}, u32[]{:S(2)}, u32[]{:S(2)}) collective-permute-start(bf16[64,16,512]{2,1,0:T(8,128)(2,1)} %copy-done.1), channel_id=1, source_target_pairs={{0,384},{128,0},{256,128},{384,256},{1,385},{129,1},{257,129},{385... | collective-permute-start | bytes 3145736 | tf_op jit(solution)/shard_map/ppermute | solution.py:275
  62.6 2.3 %collective-permute-start.1 = (bf16[64,16,512]{2,1,0:T(8,128)(2,1)}, bf16[64,16,512]{2,1,0:T(8,128)(2,1)}, u32[]{:S(2)}, u32[]{:S(2)}) collective-permute-start(bf16[64,16,512]{2,1,0:T(8,128)(2,1)} %copy-done.1), channel_id=1, source_target_pairs={{0,256},{128,384},{256,0},{384,128},{1,257},{129,385},{257,1},{385... | collective-permute-start | bytes 3145736 | tf_op jit(solution)/shard_map/ppermute | solution.py:275
  64.9 2.6 %collective-permute-start = (bf16[64,16,512]{2,1,0:T(8,128)(2,1)}, bf16[64,16,512]{2,1,0:T(8,128)(2,1)}, u32[]{:S(2)}, u32[]{:S(2)}) collective-permute-start(bf16[64,16,512]{2,1,0:T(8,128)(2,1)} %copy-done.1), channel_id=1, source_target_pairs={{0,128},{128,256},{256,384},{384,0},{1,129},{129,257},{257,385},{3... | collective-permute-start | bytes 3145736 | tf_op jit(solution)/shard_map/ppermute | solution.py:275
  67.5 5.2 %collective-permute-start.3 = (bf16[64,16,512]{2,1,0:T(8,128)(2,1)}, bf16[64,16,512]{2,1,0:T(8,128)(2,1)}, u32[]{:S(2)}, u32[]{:S(2)}) collective-permute-start(bf16[64,16,512]{2,1,0:T(8,128)(2,1)} %copy-done.1), channel_id=1, source_target_pairs={{0,1},{1,0},{2,3},{3,2},{4,5},{5,4},{6,7},{7,6},{8,9},{9,8},{10,11... | collective-permute-start | bytes 3145736 | tf_op jit(solution)/shard_map/ppermute | solution.py:278
  72.6 34.0 %collective-permute-done.2.refs_3_ = bf16[64,16,512]{2,1,0:T(8,128)(2,1)} collective-permute-done((bf16[64,16,512]{2,1,0:T(8,128)(2,1)}, bf16[64,16,512]{2,1,0:T(8,128)(2,1)}, u32[]{:S(2)}, u32[]{:S(2)}) %collective-permute-start.2) | collective-permute-done | bytes 1048608 | tf_op jit(solution)/shard_map/ppermute | solution.py:275
  106.6 6.2 %collective-permute-start.6 = (bf16[64,16,512]{2,1,0:T(8,128)(2,1)}, bf16[64,16,512]{2,1,0:T(8,128)(2,1)}, u32[]{:S(2)}, u32[]{:S(2)}) collective-permute-start(bf16[64,16,512]{2,1,0:T(8,128)(2,1)} %collective-permute-done.2.refs_3_), channel_id=1, source_target_pairs={{0,1},{1,0},{2,3},{3,2},{4,5},{5,4},{6,7},{7,6},{8,9},{9,8},{10,11... | collective-permute-start | bytes 3145736 | tf_op jit(solution)/shard_map/ppermute | solution.py:278
  112.8 0.0 collective-permute-done.1.refs_2_
  112.8 2.7 %collective-permute-start.5 = (bf16[64,16,512]{2,1,0:T(8,128)(2,1)}, bf16[64,16,512]{2,1,0:T(8,128)(2,1)}, u32[]{:S(2)}, u32[]{:S(2)}) collective-permute-start(bf16[64,16,512]{2,1,0:T(8,128)(2,1)} %collective-permute-done.1.refs_2_), channel_id=1, source_target_pairs={{0,1},{1,0},{2,3},{3,2},{4,5},{5,4},{6,7},{7,6},{8,9},{9,8},{10,11... | collective-permute-start | bytes 3145736 | tf_op jit(solution)/shard_map/ppermute | solution.py:278
  115.5 30.8 %collective-permute-done.refs_1_ = bf16[64,16,512]{2,1,0:T(8,128)(2,1)} collective-permute-done((bf16[64,16,512]{2,1,0:T(8,128)(2,1)}, bf16[64,16,512]{2,1,0:T(8,128)(2,1)}, u32[]{:S(2)}, u32[]{:S(2)}) %collective-permute-start) | collective-permute-done | bytes 1048608 | tf_op jit(solution)/shard_map/ppermute | solution.py:275
  146.4 2.3 %collective-permute-start.4 = (bf16[64,16,512]{2,1,0:T(8,128)(2,1)}, bf16[64,16,512]{2,1,0:T(8,128)(2,1)}, u32[]{:S(2)}, u32[]{:S(2)}) collective-permute-start(bf16[64,16,512]{2,1,0:T(8,128)(2,1)} %collective-permute-done.refs_1_), channel_id=1, source_target_pairs={{0,1},{1,0},{2,3},{3,2},{4,5},{5,4},{6,7},{7,6},{8,9},{9,8},{10,11... | collective-permute-start | bytes 3145736 | tf_op jit(solution)/shard_map/ppermute | solution.py:278
  148.7 0.1 pad_add_fusion.where_ref
  148.7 0.0 all-to-all-done.1
  148.8 1.2 copy-done.6
  150.0 2.2 %correct.1 = (bf16[512,256]{1,0:T(8,128)(2,1)S(1)}, bf16[512,128]{1,0:T(8,128)(2,1)S(1)}) custom-call(bf16[512,3328]{1,0:T(8,128)(2,1)S(1)} %bitcast.17, bf16[64,8192]{1,0:T(8,128)(2,1)S(1)} %bitcast.20, bf16[64,512]{1,0:T(8,128)(2,1)S(1)} %bitcast.22), custom_call_target="tpu_custom_call" | custom-call | tf_op jit(solution)/shard_map/correct/pallas_call | solution.py:284
  152.2 0.7 copy-done.10
  152.9 3.9 %grads.1 = (f32[256,1152]{1,0:T(8,128)S(1)}, bf16[256,1152]{1,0:T(8,128)(2,1)}) custom-call(s32[4]{0:T(128)S(1)} %pad_add_fusion.where_ref, bf16[512,3328]{1,0:T(8,128)(2,1)S(1)} %bitcast.18, bf16[64,512]{1,0:T(8,128)(2,1)S(1)} %bitcast.23, bf16[512,128]{1,0:T(8,128)(2,1)S(1)} %get-tuple-element.22.low_ref), custom_call_target="tpu_custom_call" | custom-call | tf_op jit(solution)/shard_map/grads/pallas_call | solution.py:299
  156.8 1.0 copy-done.4
  157.8 2.0 %collective-permute-start.7 = (bf16[256,1152]{1,0:T(8,128)(2,1)}, bf16[256,1152]{1,0:T(8,128)(2,1)S(1)}, u32[]{:S(2)}, u32[]{:S(2)}) collective-permute-start(bf16[256,1152]{1,0:T(8,128)(2,1)} %get-tuple-element.24), channel_id=1, source_target_pairs={{0,1},{1,0},{2,3},{3,2},{4,5},{5,4},{6,7},{7,6},{8,9},{9,8},{10,11... | collective-permute-start | bytes 1769480 | tf_op jit(solution)/shard_map/ppermute | solution.py:311
  159.9 14.0 %all-to-all-start.2 = ((bf16[64,8,256]{2,1,0:T(8,128)(2,1)}), bf16[64,8,256]{2,1,0:T(8,128)(2,1)S(1)}, u32[]{:S(2)}, u32[]{:S(2)}) async-start(bf16[64,8,256]{2,1,0:T(8,128)(2,1)} %bitcast.24), calls=%async_computation.2 | async-start | bytes 524288 | tf_op jit(solution)/shard_map/all_to_all | solution.py:295
  173.8 0.0 collective-permute-done.7.taken_ref
  173.8 1.3 copy-done.5
  175.1 0.7 middle.1
  175.8 4.8 %collective-permute-start.8 = (bf16[64,1152]{1,0:T(8,128)(2,1)S(1)}, bf16[64,1152]{1,0:T(8,128)(2,1)S(1)}, u32[]{:S(2)}, u32[]{:S(2)}) collective-permute-start(bf16[64,1152]{1,0:T(8,128)(2,1)S(1)} %get-tuple-element.26), channel_id=1, source_target_pairs={{0,2},{2,4},{4,6},{6,0},{1,3},{3,5},{5,7},{7,1},{8,10},{10,12},{12... | collective-permute-start | bytes 442376 | tf_op jit(solution)/shard_map/ppermute | solution.py:324
  180.6 0.0 collective-permute-done.3.refs_4_
  180.6 2.0 collective-permute-start.9
  182.6 0.0 collective-permute-done.6.refs_7_
  182.6 4.1 %collective-permute-start.10 = (bf16[64,1152]{1,0:T(8,128)(2,1)S(1)}, bf16[64,1152]{1,0:T(8,128)(2,1)S(1)}, u32[]{:S(2)}, u32[]{:S(2)}) collective-permute-start(bf16[64,1152]{1,0:T(8,128)(2,1)S(1)} %get-tuple-element.28), channel_id=1, source_target_pairs={{0,6},{2,0},{4,2},{6,4},{1,7},{3,1},{5,3},{7,5},{8,14},{10,8},{12,... | collective-permute-start | bytes 442376 | tf_op jit(solution)/shard_map/ppermute | solution.py:324
  186.7 0.0 collective-permute-done.5.refs_6_
  186.7 0.0 collective-permute-done.4.refs_5_
  186.8 1.2 copy-done.2
  188.0 10.0 %base.1.base_ref = f32[128,512]{1,0:T(8,128)S(1)} custom-call(s32[4]{0:T(128)S(1)} %pad_add_fusion.where_ref, bf16[128,8192]{1,0:T(8,128)(2,1)} %tokens_ref.3, bf16[1,512]{1,0:T(2,128)(2,1)S(1)} %reshape.25.bias_ref, bf16[64,16,512]{2,1,0:T(8,128)(2,1)S(1)} %copy-done.2, bf16[64,16,512]{2,1,0:T(8,128)(2,1)} %collective-permute-done.refs_1_, ...), custom_call_target="tpu_custom_call" | custom-call | tf_op jit(solution)/shard_map/base/pallas_call | solution.py:325
  198.0 0.9 place.1
  199.0 0.0 collective-permute-done.9.refs_1_
  199.0 0.0 collective-permute-done.10.refs_2_
  199.0 1.3 finish.1
  (20 shorter events, 0.0 us)
Async XLA Ops:
  0.6 19.1 %copy-start = (bf16[128,8192]{1,0:T(8,128)(2,1)S(1)}, bf16[128,8192]{1,0:T(8,128)(2,1)}, u32[]{:S(2)}) copy-start(bf16[128,8192]{1,0:T(8,128)(2,1)} %tokens_ref.3) | copy-start | bytes 6291460
  2.6 44.6 %all-to-all-start = ((bf16[64,16,512]{2,1,0:T(8,128)(2,1)}), bf16[64,16,512]{2,1,0:T(8,128)(2,1)S(1)}, u32[]{:S(2)}, u32[]{:S(2)}) async-start(bf16[64,16,512]{2,1,0:T(8,128)(2,1)} %broadcast_in_dim.12), calls=%async_computation | async-start | bytes 2097152 | tf_op jit(solution)/shard_map/all_to_all | solution.py:252
  19.7 0.9 copy-start.11
  20.7 0.7 copy-start.12
  21.3 0.7 copy-start.13
  27.7 1.7 copy-start.3
  29.4 0.7 copy-start.8
  47.2 1.0 copy-start.1
  47.2 101.5 %copy-start.7 = (bf16[1,64,512]{2,1,0:T(8,128)(2,1)S(1)}, bf16[1,64,512]{2,1,0:T(8,128)(2,1)}, u32[]{:S(2)}) copy-start(bf16[1,64,512]{2,1,0:T(8,128)(2,1)} %param.14) | copy-start | bytes 196612
  48.2 100.5 %all-to-all-start.1 = ((bf16[64,8,3328]{2,1,0:T(8,128)(2,1)}), bf16[64,8,3328]{2,1,0:T(8,128)(2,1)S(1)}, u32[]{:S(2)}, u32[]{:S(2)}) async-start(bf16[64,8,3328]{2,1,0:T(8,128)(2,1)} %bitcast.19), calls=%async_computation.1 | async-start | bytes 6815744 | tf_op jit(solution)/shard_map/all_to_all | solution.py:279
  58.2 48.4 %collective-permute-start.2 = (bf16[64,16,512]{2,1,0:T(8,128)(2,1)}, bf16[64,16,512]{2,1,0:T(8,128)(2,1)}, u32[]{:S(2)}, u32[]{:S(2)}) collective-permute-start(bf16[64,16,512]{2,1,0:T(8,128)(2,1)} %copy-done.1), channel_id=1, source_target_pairs={{0,384},{128,0},{256,128},{384,256},{1,385},{129,1},{257,129},{385... | collective-permute-start | bytes 3145736 | tf_op jit(solution)/shard_map/ppermute | solution.py:275
  62.6 50.2 %collective-permute-start.1 = (bf16[64,16,512]{2,1,0:T(8,128)(2,1)}, bf16[64,16,512]{2,1,0:T(8,128)(2,1)}, u32[]{:S(2)}, u32[]{:S(2)}) collective-permute-start(bf16[64,16,512]{2,1,0:T(8,128)(2,1)} %copy-done.1), channel_id=1, source_target_pairs={{0,256},{128,384},{256,0},{384,128},{1,257},{129,385},{257,1},{385... | collective-permute-start | bytes 3145736 | tf_op jit(solution)/shard_map/ppermute | solution.py:275
  64.9 81.5 %collective-permute-start = (bf16[64,16,512]{2,1,0:T(8,128)(2,1)}, bf16[64,16,512]{2,1,0:T(8,128)(2,1)}, u32[]{:S(2)}, u32[]{:S(2)}) collective-permute-start(bf16[64,16,512]{2,1,0:T(8,128)(2,1)} %copy-done.1), channel_id=1, source_target_pairs={{0,128},{128,256},{256,384},{384,0},{1,129},{129,257},{257,385},{3... | collective-permute-start | bytes 3145736 | tf_op jit(solution)/shard_map/ppermute | solution.py:275
  67.5 113.2 %collective-permute-start.3 = (bf16[64,16,512]{2,1,0:T(8,128)(2,1)}, bf16[64,16,512]{2,1,0:T(8,128)(2,1)}, u32[]{:S(2)}, u32[]{:S(2)}) collective-permute-start(bf16[64,16,512]{2,1,0:T(8,128)(2,1)} %copy-done.1), channel_id=1, source_target_pairs={{0,1},{1,0},{2,3},{3,2},{4,5},{5,4},{6,7},{7,6},{8,9},{9,8},{10,11... | collective-permute-start | bytes 3145736 | tf_op jit(solution)/shard_map/ppermute | solution.py:278
  106.6 76.0 %collective-permute-start.6 = (bf16[64,16,512]{2,1,0:T(8,128)(2,1)}, bf16[64,16,512]{2,1,0:T(8,128)(2,1)}, u32[]{:S(2)}, u32[]{:S(2)}) collective-permute-start(bf16[64,16,512]{2,1,0:T(8,128)(2,1)} %collective-permute-done.2.refs_3_), channel_id=1, source_target_pairs={{0,1},{1,0},{2,3},{3,2},{4,5},{5,4},{6,7},{7,6},{8,9},{9,8},{10,11... | collective-permute-start | bytes 3145736 | tf_op jit(solution)/shard_map/ppermute | solution.py:278
  112.8 73.9 %collective-permute-start.5 = (bf16[64,16,512]{2,1,0:T(8,128)(2,1)}, bf16[64,16,512]{2,1,0:T(8,128)(2,1)}, u32[]{:S(2)}, u32[]{:S(2)}) collective-permute-start(bf16[64,16,512]{2,1,0:T(8,128)(2,1)} %collective-permute-done.1.refs_2_), channel_id=1, source_target_pairs={{0,1},{1,0},{2,3},{3,2},{4,5},{5,4},{6,7},{7,6},{8,9},{9,8},{10,11... | collective-permute-start | bytes 3145736 | tf_op jit(solution)/shard_map/ppermute | solution.py:278
  146.4 40.4 %collective-permute-start.4 = (bf16[64,16,512]{2,1,0:T(8,128)(2,1)}, bf16[64,16,512]{2,1,0:T(8,128)(2,1)}, u32[]{:S(2)}, u32[]{:S(2)}) collective-permute-start(bf16[64,16,512]{2,1,0:T(8,128)(2,1)} %collective-permute-done.refs_1_), channel_id=1, source_target_pairs={{0,1},{1,0},{2,3},{3,2},{4,5},{5,4},{6,7},{7,6},{8,9},{9,8},{10,11... | collective-permute-start | bytes 3145736 | tf_op jit(solution)/shard_map/ppermute | solution.py:278
  148.7 1.2 copy-start.6
  152.2 0.7 copy-start.10
  152.9 33.8 %copy-start.14 = (bf16[512]{0:T(512)(128)(2,1)S(1)}, bf16[512]{0:T(512)(128)(2,1)}, u32[]{:S(2)}) copy-start(bf16[512]{0:T(512)(128)(2,1)} %param.12) | copy-start | bytes 3076
  156.8 1.0 copy-start.4
  157.8 16.0 %collective-permute-start.7 = (bf16[256,1152]{1,0:T(8,128)(2,1)}, bf16[256,1152]{1,0:T(8,128)(2,1)S(1)}, u32[]{:S(2)}, u32[]{:S(2)}) collective-permute-start(bf16[256,1152]{1,0:T(8,128)(2,1)} %get-tuple-element.24), channel_id=1, source_target_pairs={{0,1},{1,0},{2,3},{3,2},{4,5},{5,4},{6,7},{7,6},{8,9},{9,8},{10,11... | collective-permute-start | bytes 1769480 | tf_op jit(solution)/shard_map/ppermute | solution.py:311
  159.9 38.2 %all-to-all-start.2 = ((bf16[64,8,256]{2,1,0:T(8,128)(2,1)}), bf16[64,8,256]{2,1,0:T(8,128)(2,1)S(1)}, u32[]{:S(2)}, u32[]{:S(2)}) async-start(bf16[64,8,256]{2,1,0:T(8,128)(2,1)} %bitcast.24), calls=%async_computation.2 | async-start | bytes 524288 | tf_op jit(solution)/shard_map/all_to_all | solution.py:295
  173.8 1.3 copy-start.5
  175.8 23.2 %collective-permute-start.8 = (bf16[64,1152]{1,0:T(8,128)(2,1)S(1)}, bf16[64,1152]{1,0:T(8,128)(2,1)S(1)}, u32[]{:S(2)}, u32[]{:S(2)}) collective-permute-start(bf16[64,1152]{1,0:T(8,128)(2,1)S(1)} %get-tuple-element.26), channel_id=1, source_target_pairs={{0,2},{2,4},{4,6},{6,0},{1,3},{3,5},{5,7},{7,1},{8,10},{10,12},{12... | collective-permute-start | bytes 442376 | tf_op jit(solution)/shard_map/ppermute | solution.py:324
  180.6 18.3 %collective-permute-start.9 = (bf16[64,1152]{1,0:T(8,128)(2,1)S(1)}, bf16[64,1152]{1,0:T(8,128)(2,1)S(1)}, u32[]{:S(2)}, u32[]{:S(2)}) collective-permute-start(bf16[64,1152]{1,0:T(8,128)(2,1)S(1)} %get-tuple-element.27), channel_id=1, source_target_pairs={{0,4},{2,6},{4,0},{6,2},{1,5},{3,7},{5,1},{7,3},{8,12},{10,14},{12... | collective-permute-start | bytes 442376 | tf_op jit(solution)/shard_map/ppermute | solution.py:324
  182.6 16.3 %collective-permute-start.10 = (bf16[64,1152]{1,0:T(8,128)(2,1)S(1)}, bf16[64,1152]{1,0:T(8,128)(2,1)S(1)}, u32[]{:S(2)}, u32[]{:S(2)}) collective-permute-start(bf16[64,1152]{1,0:T(8,128)(2,1)S(1)} %get-tuple-element.28), channel_id=1, source_target_pairs={{0,6},{2,0},{4,2},{6,4},{1,7},{3,1},{5,3},{7,5},{8,14},{10,8},{12,... | collective-permute-start | bytes 442376 | tf_op jit(solution)/shard_map/ppermute | solution.py:324
  186.8 1.2 copy-start.2
  188.0 10.0 %copy-start.9 = (bf16[2,512,128]{2,1,0:T(8,128)(2,1)S(1)}, bf16[2,512,128]{2,1,0:T(8,128)(2,1)}, u32[]{:S(2)}) copy-start(bf16[2,512,128]{2,1,0:T(8,128)(2,1)} %copy-done.8) | copy-start | bytes 786436

commit v5 on v4

--- a/solution.py
+++ b/solution.py
@@ -115,10 +115,11 @@
     back_ref[...] = nn(low, stacked_up(up_ref)).astype(BF16)
 
 
-def grads_kernel(where_ref, arrived_ref, up_ref, low_ref, keep_ref, give_ref, grad_ref):
+def grads_kernel(where_ref, arrived_ref, up_ref, low_ref, keep_ref, give_ref):
     rows = arrived_ref.shape[0]
     rank = up_ref.shape[0]
-    chunk = grad_ref.shape[1] - 2 * rank
+    chunk = keep_ref.shape[1] - 2 * rank
+    first = where_ref[3] == 0
     cot = arrived_ref[:, SLOTS * chunk :]
     q = iota((rows, 2 * rank), 0) % Q
     part = iota((rows, 2 * rank), 1) // rank
@@ -132,6 +133,12 @@
         )
     left = jnp.concatenate(lefts, axis=0)
     step = 256
+
+    def put(low, high, y, columns):
+        block = slice(y * rank, (y + 1) * rank)
+        keep_ref[block, columns] = jnp.where(first, low, high)
+        give_ref[block, columns] = jnp.where(first, high, low).astype(BF16)
+
     for start in range(0, chunk, step):
         right = jnp.concatenate(
             [
@@ -140,22 +147,17 @@
             ],
             axis=0,
         )
-        grad_ref[:, start : start + step] = tn(left, right)
+        both = tn(left, right).reshape(Q // 2, 2, rank, step)
+        for y in range(Q // 2):
+            put(both[y, 0], both[y, 1], y, slice(start, start + step))
     up = tn(low_ref[...], cot)
     per_half = Q // 2
-    for d in range(Q):
-        column = (d % per_half) // 2 * 2 * rank
-        first = d // per_half * rank
-        grad_ref[d * rank : (d + 1) * rank, chunk:] = up[
-            first : first + rank, column : column + 2 * rank
-        ]
-    core = where_ref[3]
     for y in range(Q // 2):
-        block = slice(y * rank, (y + 1) * rank)
-        keep_ref[block] = grad_ref[pl.ds(pl.multiple_of((2 * y + core) * rank, rank), rank)]
-        give_ref[block] = grad_ref[
-            pl.ds(pl.multiple_of((2 * y + 1 - core) * rank, rank), rank)
-        ].astype(BF16)
+        d = 2 * y
+        column = d % per_half * rank
+        row = d // per_half * rank
+        part = up[row : row + rank, column : column + 2 * rank]
+        put(part, part, y, slice(chunk, chunk + 2 * rank))
 
 
 def middle_kernel(where_ref, keep_ref, taken_ref, mine_ref, *sent_refs):
@@ -216,11 +218,19 @@
         values_ref[:, columns] = (base_ref[:, columns] + placed).astype(BF16)
 
 
+def spread_kernel(weight_ref, spread_ref, held_ref, sem):
+    held_ref[...] = jnp.broadcast_to(weight_ref[...][None], held_ref.shape)
+    copy = pltpu.make_async_copy(held_ref, spread_ref, sem)
+    copy.start()
+    copy.wait()
+
+
 def vmem(number):
     return [pl.BlockSpec(memory_space=pltpu.VMEM)] * number
 
 
-PARAMS = pltpu.CompilerParams(vmem_limit_bytes=48 << 20)
+ANY = pl.BlockSpec(memory_space=pl.ANY)
+PARAMS = pltpu.CompilerParams(vmem_limit_bytes=24 << 20)
 
 
 def body(
@@ -236,7 +246,6 @@
     count, width = tokens.shape
     out_width = frozen_value_weight.shape[1]
     fsdp = lax.axis_size(FSDP)
-    dp = lax.axis_size(DP)
     size_x = lax.axis_size("x")
     size_z = lax.axis_size("z")
     size_y = lax.axis_size("yl")
@@ -249,8 +258,17 @@
     columns = SLOTS * chunk + half
 
     plane = lax.axis_size(PLANE)
+    spread = (plane, *frozen_value_weight.shape)
     piece = lax.all_to_all(
-        jnp.broadcast_to(frozen_value_weight[None], (plane, *frozen_value_weight.shape)),
+        pl.pallas_call(
+            spread_kernel,
+            out_shape=jax.ShapeDtypeStruct(spread, BF16),
+            in_specs=vmem(1),
+            out_specs=ANY,
+            scratch_shapes=[pltpu.VMEM(spread, BF16), pltpu.SemaphoreType.DMA],
+            compiler_params=PARAMS,
+            name="spread",
+        )(frozen_value_weight),
         PLANE,
         split_axis=0,
         concat_axis=0,
@@ -304,7 +322,6 @@
         ),
         in_specs=smem + vmem(3),
         out_specs=tuple(vmem(2)),
-        scratch_shapes=[pltpu.VMEM((dp * rank, wide), F32)],
         compiler_params=PARAMS,
         name="grads",
     )(where, arrived, up, low)

time: 202 us -> 203 us (level)
    unnamed x30 -> x36, local copies, waits for them, and re-layouts: 11 us -> 14.5 us
  transfers between devices with their start and end apart: 14 -> 14, of which waited for: 3 -> 3; matrix products, arithmetic and copies ran while one was open for 0% -> 0% of each run, Pallas kernels for 12% -> 11%
where the time goes in v5:
time: 203 us; the launch traced here: 201 us
  waiting for transfers between devices  81.9 us (40%)
  starting transfers between devices  79.5 us (39%)
  Pallas kernels  24.2 us (12%)
  local copies, waits for them, and re-layouts  14.5 us (7%)
    ppermute x3, waiting for transfers between devices, body(): own.append(lax.ppermute(piece, 'x', shift))  64.8 us
    all_to_all x1, starting transfers between devices, body(): lax.all_to_all(pl.pallas_call(spread_kernel, out_shape=jax.ShapeDtypeStru...  17.1 us
    all_to_all x1, waiting for transfers between devices, body(): lax.all_to_all(pl.pallas_call(spread_kernel, out_shape=jax.ShapeDtypeStru...  17.1 us
    ppermute x4, starting transfers between devices, body(): other.append(lax.ppermute(own[k], 'core', SWAP))  16.4 us
    unnamed x36, local copies, waits for them, and re-layouts  14.5 us
    all_to_all x1, starting transfers between devices, body(): lax.all_to_all(back.reshape(fsdp, Q, half), FSDP, split_axis=0, concat_ax...  13.9 us
    ppermute x3, starting transfers between devices, body(): arrivals.append(lax.ppermute(sums[k - 1], 'yl', rise))  10.9 us
    all_to_all x1, starting transfers between devices, body(): lax.all_to_all(sent.reshape(fsdp, Q, columns), FSDP, split_axis=0, concat...  10 us
  transfers between devices with their start and end apart: 14, of which 3 were waited for; matrix products, arithmetic and copies ran while one was open for 0% of the time, Pallas kernels for 11%

profile of v5, /device:TPU:1, one launch (start us, length us, event | category | flops | bytes accessed | tf_op | source)
XLA Modules:
  0.0 201.1 jit_solution(13273091688565288867)
XLA Ops:
  0.6 0.0 copy-start
  0.7 0.9 copy-done.14
  1.5 0.2 spread.1
  1.7 1.0 copy-done.4
  2.7 17.1 %all-to-all-start = ((bf16[64,16,512]{2,1,0:T(8,128)(2,1)}), bf16[64,16,512]{2,1,0:T(8,128)(2,1)S(1)}, u32[]{:S(2)}, u32[]{:S(2)}) async-start(bf16[64,16,512]{2,1,0:T(8,128)(2,1)} %copy-done.4), calls=%async_computation | async-start | bytes 2097152 | tf_op jit(solution)/shard_map/all_to_all | solution.py:262
  19.9 0.0 copy-start.13
  19.9 0.9 copy-done.13
  20.8 0.7 copy-done.15
  21.4 0.7 copy-done.16
  22.1 5.8 %dispatch.1 = (bf16[512,3328]{1,0:T(8,128)(2,1)S(1)}, bf16[2,512,128]{2,1,0:T(8,128)(2,1)S(1)}) custom-call(s32[64]{0:T(128)S(1)} %copy-done.15, s32[1,128]{1,0:T(1,128)S(1)} %bitcast.25, bf16[128,8192]{1,0:T(8,128)(2,1)S(1)} %copy-done, bf16[128,512]{1,0:T(8,128)(2,1)S(1)} %copy-done.13), custom_call_target="tpu_custom_call" | custom-call | tf_op jit(solution)/shard_map/dispatch/pallas_call | solution.py:277
  27.9 1.7 copy-done.5
  29.6 0.7 copy-done.10
  30.3 17.1 %all-to-all-done.refs_0_ = bf16[64,16,512]{2,1,0:T(8,128)(2,1)S(1)} async-done(((bf16[64,16,512]{2,1,0:T(8,128)(2,1)}), bf16[64,16,512]{2,1,0:T(8,128)(2,1)S(1)}, u32[]{:S(2)}, u32[]{:S(2)}) %all-to-all-start) | async-done | bytes 1048608 | tf_op jit(solution)/shard_map/all_to_all | solution.py:262
  47.3 1.0 copy-done.2
  48.3 10.0 %all-to-all-start.1 = ((bf16[64,8,3328]{2,1,0:T(8,128)(2,1)}), bf16[64,8,3328]{2,1,0:T(8,128)(2,1)S(1)}, u32[]{:S(2)}, u32[]{:S(2)}) async-start(bf16[64,8,3328]{2,1,0:T(8,128)(2,1)} %bitcast.19), calls=%async_computation.1 | async-start | bytes 6815744 | tf_op jit(solution)/shard_map/all_to_all | solution.py:297
  58.4 4.3 %collective-permute-start.2 = (bf16[64,16,512]{2,1,0:T(8,128)(2,1)}, bf16[64,16,512]{2,1,0:T(8,128)(2,1)}, u32[]{:S(2)}, u32[]{:S(2)}) collective-permute-start(bf16[64,16,512]{2,1,0:T(8,128)(2,1)} %copy-done.2), channel_id=1, source_target_pairs={{0,384},{128,0},{256,128},{384,256},{1,385},{129,1},{257,129},{385... | collective-permute-start | bytes 3145736 | tf_op jit(solution)/shard_map/ppermute | solution.py:293
  62.7 2.3 %collective-permute-start.1 = (bf16[64,16,512]{2,1,0:T(8,128)(2,1)}, bf16[64,16,512]{2,1,0:T(8,128)(2,1)}, u32[]{:S(2)}, u32[]{:S(2)}) collective-permute-start(bf16[64,16,512]{2,1,0:T(8,128)(2,1)} %copy-done.2), channel_id=1, source_target_pairs={{0,256},{128,384},{256,0},{384,128},{1,257},{129,385},{257,1},{385... | collective-permute-start | bytes 3145736 | tf_op jit(solution)/shard_map/ppermute | solution.py:293
  65.0 2.6 %collective-permute-start = (bf16[64,16,512]{2,1,0:T(8,128)(2,1)}, bf16[64,16,512]{2,1,0:T(8,128)(2,1)}, u32[]{:S(2)}, u32[]{:S(2)}) collective-permute-start(bf16[64,16,512]{2,1,0:T(8,128)(2,1)} %copy-done.2), channel_id=1, source_target_pairs={{0,128},{128,256},{256,384},{384,0},{1,129},{129,257},{257,385},{3... | collective-permute-start | bytes 3145736 | tf_op jit(solution)/shard_map/ppermute | solution.py:293
  67.6 5.2 %collective-permute-start.3 = (bf16[64,16,512]{2,1,0:T(8,128)(2,1)}, bf16[64,16,512]{2,1,0:T(8,128)(2,1)}, u32[]{:S(2)}, u32[]{:S(2)}) collective-permute-start(bf16[64,16,512]{2,1,0:T(8,128)(2,1)} %copy-done.2), channel_id=1, source_target_pairs={{0,1},{1,0},{2,3},{3,2},{4,5},{5,4},{6,7},{7,6},{8,9},{9,8},{10,11... | collective-permute-start | bytes 3145736 | tf_op jit(solution)/shard_map/ppermute | solution.py:296
  72.8 34.0 %collective-permute-done.2.refs_3_ = bf16[64,16,512]{2,1,0:T(8,128)(2,1)} collective-permute-done((bf16[64,16,512]{2,1,0:T(8,128)(2,1)}, bf16[64,16,512]{2,1,0:T(8,128)(2,1)}, u32[]{:S(2)}, u32[]{:S(2)}) %collective-permute-start.2) | collective-permute-done | bytes 1048608 | tf_op jit(solution)/shard_map/ppermute | solution.py:293
  106.7 6.2 %collective-permute-start.6 = (bf16[64,16,512]{2,1,0:T(8,128)(2,1)}, bf16[64,16,512]{2,1,0:T(8,128)(2,1)}, u32[]{:S(2)}, u32[]{:S(2)}) collective-permute-start(bf16[64,16,512]{2,1,0:T(8,128)(2,1)} %collective-permute-done.2.refs_3_), channel_id=1, source_target_pairs={{0,1},{1,0},{2,3},{3,2},{4,5},{5,4},{6,7},{7,6},{8,9},{9,8},{10,11... | collective-permute-start | bytes 3145736 | tf_op jit(solution)/shard_map/ppermute | solution.py:296
  112.9 0.0 collective-permute-done.1.refs_2_
  112.9 2.7 %collective-permute-start.5 = (bf16[64,16,512]{2,1,0:T(8,128)(2,1)}, bf16[64,16,512]{2,1,0:T(8,128)(2,1)}, u32[]{:S(2)}, u32[]{:S(2)}) collective-permute-start(bf16[64,16,512]{2,1,0:T(8,128)(2,1)} %collective-permute-done.1.refs_2_), channel_id=1, source_target_pairs={{0,1},{1,0},{2,3},{3,2},{4,5},{5,4},{6,7},{7,6},{8,9},{9,8},{10,11... | collective-permute-start | bytes 3145736 | tf_op jit(solution)/shard_map/ppermute | solution.py:296
  115.6 30.8 %collective-permute-done.refs_1_ = bf16[64,16,512]{2,1,0:T(8,128)(2,1)} collective-permute-done((bf16[64,16,512]{2,1,0:T(8,128)(2,1)}, bf16[64,16,512]{2,1,0:T(8,128)(2,1)}, u32[]{:S(2)}, u32[]{:S(2)}) %collective-permute-start) | collective-permute-done | bytes 1048608 | tf_op jit(solution)/shard_map/ppermute | solution.py:293
  146.5 2.3 %collective-permute-start.4 = (bf16[64,16,512]{2,1,0:T(8,128)(2,1)}, bf16[64,16,512]{2,1,0:T(8,128)(2,1)}, u32[]{:S(2)}, u32[]{:S(2)}) collective-permute-start(bf16[64,16,512]{2,1,0:T(8,128)(2,1)} %collective-permute-done.refs_1_), channel_id=1, source_target_pairs={{0,1},{1,0},{2,3},{3,2},{4,5},{5,4},{6,7},{7,6},{8,9},{9,8},{10,11... | collective-permute-start | bytes 3145736 | tf_op jit(solution)/shard_map/ppermute | solution.py:296
  148.8 0.1 pad_add_fusion.where_ref
  148.9 1.2 copy-done.8
  150.1 2.2 %correct.1 = (bf16[512,256]{1,0:T(8,128)(2,1)S(1)}, bf16[512,128]{1,0:T(8,128)(2,1)S(1)}) custom-call(bf16[512,3328]{1,0:T(8,128)(2,1)S(1)} %bitcast.17, bf16[64,8192]{1,0:T(8,128)(2,1)S(1)} %bitcast.20, bf16[64,512]{1,0:T(8,128)(2,1)S(1)} %bitcast.22), custom_call_target="tpu_custom_call" | custom-call | tf_op jit(solution)/shard_map/correct/pallas_call | solution.py:302
  152.3 0.7 copy-done.12
  153.0 3.7 %grads.1 = (f32[256,1152]{1,0:T(8,128)S(1)}, bf16[256,1152]{1,0:T(8,128)(2,1)}) custom-call(s32[4]{0:T(128)S(1)} %pad_add_fusion.where_ref, bf16[512,3328]{1,0:T(8,128)(2,1)S(1)} %bitcast.18, bf16[64,512]{1,0:T(8,128)(2,1)S(1)} %bitcast.23, bf16[512,128]{1,0:T(8,128)(2,1)S(1)} %get-tuple-element.22.low_ref), custom_call_target="tpu_custom_call" | custom-call | tf_op jit(solution)/shard_map/grads/pallas_call | solution.py:317
  156.7 1.0 copy-done.6
  157.8 2.0 collective-permute-start.7
  159.8 13.9 %all-to-all-start.2 = ((bf16[64,8,256]{2,1,0:T(8,128)(2,1)}), bf16[64,8,256]{2,1,0:T(8,128)(2,1)S(1)}, u32[]{:S(2)}, u32[]{:S(2)}) async-start(bf16[64,8,256]{2,1,0:T(8,128)(2,1)} %bitcast.24), calls=%async_computation.2 | async-start | bytes 524288 | tf_op jit(solution)/shard_map/all_to_all | solution.py:313
  173.8 1.3 copy-done.7
  175.0 0.6 middle.1
  175.7 4.8 %collective-permute-start.8 = (bf16[64,1152]{1,0:T(8,128)(2,1)S(1)}, bf16[64,1152]{1,0:T(8,128)(2,1)S(1)}, u32[]{:S(2)}, u32[]{:S(2)}) collective-permute-start(bf16[64,1152]{1,0:T(8,128)(2,1)S(1)} %get-tuple-element.26), channel_id=1, source_target_pairs={{0,2},{2,4},{4,6},{6,0},{1,3},{3,5},{5,7},{7,1},{8,10},{10,12},{12... | collective-permute-start | bytes 442376 | tf_op jit(solution)/shard_map/ppermute | solution.py:341
  180.5 2.0 collective-permute-start.9
  182.5 4.1 %collective-permute-start.10 = (bf16[64,1152]{1,0:T(8,128)(2,1)S(1)}, bf16[64,1152]{1,0:T(8,128)(2,1)S(1)}, u32[]{:S(2)}, u32[]{:S(2)}) collective-permute-start(bf16[64,1152]{1,0:T(8,128)(2,1)S(1)} %get-tuple-element.28), channel_id=1, source_target_pairs={{0,6},{2,0},{4,2},{6,4},{1,7},{3,1},{5,3},{7,5},{8,14},{10,8},{12,... | collective-permute-start | bytes 442376 | tf_op jit(solution)/shard_map/ppermute | solution.py:341
  186.6 0.0 collective-permute-done.5.refs_6_
  186.6 0.0 collective-permute-done.4.refs_5_
  186.7 0.0 copy-start.1
  186.7 1.6 copy-done.1
  188.3 1.2 copy-done.3
  189.5 9.4 %base.1.base_ref = f32[128,512]{1,0:T(8,128)S(1)} custom-call(s32[4]{0:T(128)S(1)} %pad_add_fusion.where_ref, bf16[128,8192]{1,0:T(8,128)(2,1)S(1)} %copy-done.1, bf16[1,512]{1,0:T(2,128)(2,1)S(1)} %reshape.24.bias_ref, bf16[64,16,512]{2,1,0:T(8,128)(2,1)S(1)} %copy-done.3, bf16[64,16,512]{2,1,0:T(8,128)(2,1)} %collective-permute-done.refs_1_, ...), custom_call_target="tpu_custom_call" | custom-call | tf_op jit(solution)/shard_map/base/pallas_call | solution.py:342
  198.9 0.9 place.1
  199.8 0.0 collective-permute-done.9.refs_1_
  199.8 0.0 collective-permute-done.10.refs_2_
  199.8 1.3 finish.1
  (26 shorter events, 0.1 us)
Async XLA Ops:
  0.6 19.2 %copy-start = (bf16[128,8192]{1,0:T(8,128)(2,1)S(1)}, bf16[128,8192]{1,0:T(8,128)(2,1)}, u32[]{:S(2)}) copy-start(bf16[128,8192]{1,0:T(8,128)(2,1)} %tokens_ref.3) | copy-start | bytes 6291460
  0.6 0.9 copy-start.14
  1.7 1.0 copy-start.4
  2.7 44.6 %all-to-all-start = ((bf16[64,16,512]{2,1,0:T(8,128)(2,1)}), bf16[64,16,512]{2,1,0:T(8,128)(2,1)S(1)}, u32[]{:S(2)}, u32[]{:S(2)}) async-start(bf16[64,16,512]{2,1,0:T(8,128)(2,1)} %copy-done.4), calls=%async_computation | async-start | bytes 2097152 | tf_op jit(solution)/shard_map/all_to_all | solution.py:262
  19.9 0.9 copy-start.13
  20.8 0.7 copy-start.15
  21.4 0.7 copy-start.16
  27.9 1.7 copy-start.5
  29.6 0.7 copy-start.10
  47.3 1.0 copy-start.2
  47.3 101.5 %copy-start.9 = (bf16[1,64,512]{2,1,0:T(8,128)(2,1)S(1)}, bf16[1,64,512]{2,1,0:T(8,128)(2,1)}, u32[]{:S(2)}) copy-start(bf16[1,64,512]{2,1,0:T(8,128)(2,1)} %param.14) | copy-start | bytes 196612
  48.3 100.5 %all-to-all-start.1 = ((bf16[64,8,3328]{2,1,0:T(8,128)(2,1)}), bf16[64,8,3328]{2,1,0:T(8,128)(2,1)S(1)}, u32[]{:S(2)}, u32[]{:S(2)}) async-start(bf16[64,8,3328]{2,1,0:T(8,128)(2,1)} %bitcast.19), calls=%async_computation.1 | async-start | bytes 6815744 | tf_op jit(solution)/shard_map/all_to_all | solution.py:297
  58.4 48.4 %collective-permute-start.2 = (bf16[64,16,512]{2,1,0:T(8,128)(2,1)}, bf16[64,16,512]{2,1,0:T(8,128)(2,1)}, u32[]{:S(2)}, u32[]{:S(2)}) collective-permute-start(bf16[64,16,512]{2,1,0:T(8,128)(2,1)} %copy-done.2), channel_id=1, source_target_pairs={{0,384},{128,0},{256,128},{384,256},{1,385},{129,1},{257,129},{385... | collective-permute-start | bytes 3145736 | tf_op jit(solution)/shard_map/ppermute | solution.py:293
  62.7 50.2 %collective-permute-start.1 = (bf16[64,16,512]{2,1,0:T(8,128)(2,1)}, bf16[64,16,512]{2,1,0:T(8,128)(2,1)}, u32[]{:S(2)}, u32[]{:S(2)}) collective-permute-start(bf16[64,16,512]{2,1,0:T(8,128)(2,1)} %copy-done.2), channel_id=1, source_target_pairs={{0,256},{128,384},{256,0},{384,128},{1,257},{129,385},{257,1},{385... | collective-permute-start | bytes 3145736 | tf_op jit(solution)/shard_map/ppermute | solution.py:293
  65.0 81.5 %collective-permute-start = (bf16[64,16,512]{2,1,0:T(8,128)(2,1)}, bf16[64,16,512]{2,1,0:T(8,128)(2,1)}, u32[]{:S(2)}, u32[]{:S(2)}) collective-permute-start(bf16[64,16,512]{2,1,0:T(8,128)(2,1)} %copy-done.2), channel_id=1, source_target_pairs={{0,128},{128,256},{256,384},{384,0},{1,129},{129,257},{257,385},{3... | collective-permute-start | bytes 3145736 | tf_op jit(solution)/shard_map/ppermute | solution.py:293
  67.6 112.9 %collective-permute-start.3 = (bf16[64,16,512]{2,1,0:T(8,128)(2,1)}, bf16[64,16,512]{2,1,0:T(8,128)(2,1)}, u32[]{:S(2)}, u32[]{:S(2)}) collective-permute-start(bf16[64,16,512]{2,1,0:T(8,128)(2,1)} %copy-done.2), channel_id=1, source_target_pairs={{0,1},{1,0},{2,3},{3,2},{4,5},{5,4},{6,7},{7,6},{8,9},{9,8},{10,11... | collective-permute-start | bytes 3145736 | tf_op jit(solution)/shard_map/ppermute | solution.py:296
  106.7 75.8 %collective-permute-start.6 = (bf16[64,16,512]{2,1,0:T(8,128)(2,1)}, bf16[64,16,512]{2,1,0:T(8,128)(2,1)}, u32[]{:S(2)}, u32[]{:S(2)}) collective-permute-start(bf16[64,16,512]{2,1,0:T(8,128)(2,1)} %collective-permute-done.2.refs_3_), channel_id=1, source_target_pairs={{0,1},{1,0},{2,3},{3,2},{4,5},{5,4},{6,7},{7,6},{8,9},{9,8},{10,11... | collective-permute-start | bytes 3145736 | tf_op jit(solution)/shard_map/ppermute | solution.py:296
  112.9 73.7 %collective-permute-start.5 = (bf16[64,16,512]{2,1,0:T(8,128)(2,1)}, bf16[64,16,512]{2,1,0:T(8,128)(2,1)}, u32[]{:S(2)}, u32[]{:S(2)}) collective-permute-start(bf16[64,16,512]{2,1,0:T(8,128)(2,1)} %collective-permute-done.1.refs_2_), channel_id=1, source_target_pairs={{0,1},{1,0},{2,3},{3,2},{4,5},{5,4},{6,7},{7,6},{8,9},{9,8},{10,11... | collective-permute-start | bytes 3145736 | tf_op jit(solution)/shard_map/ppermute | solution.py:296
  146.5 40.2 %collective-permute-start.4 = (bf16[64,16,512]{2,1,0:T(8,128)(2,1)}, bf16[64,16,512]{2,1,0:T(8,128)(2,1)}, u32[]{:S(2)}, u32[]{:S(2)}) collective-permute-start(bf16[64,16,512]{2,1,0:T(8,128)(2,1)} %collective-permute-done.refs_1_), channel_id=1, source_target_pairs={{0,1},{1,0},{2,3},{3,2},{4,5},{5,4},{6,7},{7,6},{8,9},{9,8},{10,11... | collective-permute-start | bytes 3145736 | tf_op jit(solution)/shard_map/ppermute | solution.py:296
  148.9 1.2 copy-start.8
  152.3 0.7 copy-start.12
  153.0 33.6 %copy-start.17 = (bf16[512]{0:T(512)(128)(2,1)S(1)}, bf16[512]{0:T(512)(128)(2,1)}, u32[]{:S(2)}) copy-start(bf16[512]{0:T(512)(128)(2,1)} %param.12) | copy-start | bytes 3076
  156.7 1.0 copy-start.6
  157.8 16.0 %collective-permute-start.7 = (bf16[256,1152]{1,0:T(8,128)(2,1)}, bf16[256,1152]{1,0:T(8,128)(2,1)S(1)}, u32[]{:S(2)}, u32[]{:S(2)}) collective-permute-start(bf16[256,1152]{1,0:T(8,128)(2,1)} %get-tuple-element.24), channel_id=1, source_target_pairs={{0,1},{1,0},{2,3},{3,2},{4,5},{5,4},{6,7},{7,6},{8,9},{9,8},{10,11... | collective-permute-start | bytes 1769480 | tf_op jit(solution)/shard_map/ppermute | solution.py:328
  159.8 39.1 %all-to-all-start.2 = ((bf16[64,8,256]{2,1,0:T(8,128)(2,1)}), bf16[64,8,256]{2,1,0:T(8,128)(2,1)S(1)}, u32[]{:S(2)}, u32[]{:S(2)}) async-start(bf16[64,8,256]{2,1,0:T(8,128)(2,1)} %bitcast.24), calls=%async_computation.2 | async-start | bytes 524288 | tf_op jit(solution)/shard_map/all_to_all | solution.py:313
  173.8 1.3 copy-start.7
  175.7 24.1 %collective-permute-start.8 = (bf16[64,1152]{1,0:T(8,128)(2,1)S(1)}, bf16[64,1152]{1,0:T(8,128)(2,1)S(1)}, u32[]{:S(2)}, u32[]{:S(2)}) collective-permute-start(bf16[64,1152]{1,0:T(8,128)(2,1)S(1)} %get-tuple-element.26), channel_id=1, source_target_pairs={{0,2},{2,4},{4,6},{6,0},{1,3},{3,5},{5,7},{7,1},{8,10},{10,12},{12... | collective-permute-start | bytes 442376 | tf_op jit(solution)/shard_map/ppermute | solution.py:341
  180.5 19.3 %collective-permute-start.9 = (bf16[64,1152]{1,0:T(8,128)(2,1)S(1)}, bf16[64,1152]{1,0:T(8,128)(2,1)S(1)}, u32[]{:S(2)}, u32[]{:S(2)}) collective-permute-start(bf16[64,1152]{1,0:T(8,128)(2,1)S(1)} %get-tuple-element.27), channel_id=1, source_target_pairs={{0,4},{2,6},{4,0},{6,2},{1,5},{3,7},{5,1},{7,3},{8,12},{10,14},{12... | collective-permute-start | bytes 442376 | tf_op jit(solution)/shard_map/ppermute | solution.py:341
  182.5 17.3 %collective-permute-start.10 = (bf16[64,1152]{1,0:T(8,128)(2,1)S(1)}, bf16[64,1152]{1,0:T(8,128)(2,1)S(1)}, u32[]{:S(2)}, u32[]{:S(2)}) collective-permute-start(bf16[64,1152]{1,0:T(8,128)(2,1)S(1)} %get-tuple-element.28), channel_id=1, source_target_pairs={{0,6},{2,0},{4,2},{6,4},{1,7},{3,1},{5,3},{7,5},{8,14},{10,8},{12,... | collective-permute-start | bytes 442376 | tf_op jit(solution)/shard_map/ppermute | solution.py:341
  186.7 1.6 copy-start.1
  188.3 1.2 copy-start.3
  189.5 9.4 %copy-start.11 = (bf16[2,512,128]{2,1,0:T(8,128)(2,1)S(1)}, bf16[2,512,128]{2,1,0:T(8,128)(2,1)}, u32[]{:S(2)}) copy-start(bf16[2,512,128]{2,1,0:T(8,128)(2,1)} %copy-done.10) | copy-start | bytes 786436
